TPU v7x, 128 devices: a whole 4x4x4 slice. The times are simulated.
128 devices in a mesh: param: 16 (over x, y_hi, core), ex: 8 (over y_lo, z).
Axes of the slice: x: 4, y: 4 (y_hi: 2, y_lo: 2; y = y_hi * 2 + y_lo), z: 4, core: 2. Of those that a mesh axis runs over, the one named last changes fastest.
Arguments:
- grads: float32 [98304, 4096], P('param', 'ex'), may hold values from -6 to 6
- projection: bfloat16 [98304, 1024], P('param'), may hold values from -6 to 6
- whitener: float32 [1024, 1024], P('param'), may hold values from -1 to 3
Outputs:
- scores: float32 [4096, 4096], P('ex', 'param')
All inputs are finite; a program needn't handle non-finite values.
Results may differ from a plain program's by a relative error of at most 0.0052.
Values may be sent and summed in bfloat16 or wider, within the bound.
No kernel may reach another device: no remote copies, remote signals or barrier semaphores. Data moves between devices by JAX's collectives and lax.ppermute only.
A program may use at most 128 MiB of HBM per device.

v0:
```python
import math

import jax
import jax.numpy as jnp
from jax import lax
from jax.sharding import PartitionSpec as P


def body(grads, projection, whitener):
    low_grads = grads.astype(jnp.bfloat16)
    partial_value = lax.dot_general(
        projection, low_grads, (((0,), (0,)), ((), ())), preferred_element_type=jnp.float32
    )
    param_count = lax.axis_size("param")
    ex_count = lax.axis_size("ex")
    norm_factor = 1.0 / math.sqrt(grads.shape[0] * param_count)
    whole_whitener = lax.all_gather(whitener, "param", axis=0, tiled=True)
    sketch_rows = partial_value.shape[0]
    local_width = grads.shape[1]
    total_width = local_width * ex_count
    tile_width = total_width // param_count
    col_start = lax.axis_index("param") * tile_width
    sketch = lax.psum(partial_value, "param") * norm_factor
    whitened = jnp.dot(whole_whitener, sketch, precision=lax.Precision.HIGHEST).astype(jnp.bfloat16)
    all_columns = lax.all_gather(whitened, "ex", axis=1, tiled=True)
    row_start = lax.axis_index("ex") * local_width
    row_block = lax.dynamic_slice_in_dim(all_columns, row_start, local_width, 1)
    col_block = lax.dynamic_slice_in_dim(all_columns, col_start, tile_width, 1)
    tile = lax.dot_general(
        row_block, col_block, (((0,), (0,)), ((), ())), preferred_element_type=jnp.float32
    )
    return tile / sketch_rows


def solution(mesh):
    return jax.shard_map(
        body,
        mesh=mesh,
        in_specs=(P("param", "ex"), P("param", None), P("param", None)),
        out_specs=P("ex", "param"),
        check_vma=False,
    )
```

profile of v0, /device:TPU:1, one launch (start us, length us, event | category | flops | bytes accessed | tf_op | source)
XLA Modules:
  0.0 344.9 jit_solution(1237545374964463168)
XLA Ops:
  6.5 0.0 all-reduce.2.cloned.1.call-start
  6.5 14.3 %fusion = f32[1024,512]{1,0:T(8,128)} fusion(bf16[6144,1024]{1,0:T(8,128)(2,1)} %param.4, f32[6144,512]{1,0:T(8,128)} %param.3), kind=kOutput, calls=%fused_computation | convolution fusion | flops 6445596672 | bytes 27262976 | tf_op jit(solution)/shard_map/dot_general | solution.py:11
  20.9 0.0 all-reduce.2.cloned.1.call-update
  20.9 0.0 all-gather.3.cloned.1.call-start
  21.0 0.7 all-gather.3.cloned.1.call-update
  21.7 0.0 all-gather.5.cloned.1.call-start
  21.7 146.6 %all-reduce.2.cloned.1.call-done = f32[1024,512]{1,0:T(8,128)} async-done(((f32[1024,512]{1,0:T(8,128)}), f32[1024,512]{1,0:T(8,128)}) %all-reduce.2.cloned.1.call-update) | async-done | bytes 2097168 | tf_op jit(solution)/shard_map/psum | solution.py:23
  168.3 60.1 %all-gather.3.cloned.1.call-done = f32[1024,1024]{1,0:T(8,128)} async-done(((f32[64,1024]{1,0:T(8,128)}), f32[1024,1024]{1,0:T(8,128)}) %all-gather.3.cloned.1.call-update) | async-done | bytes 4194320 | tf_op jit(solution)/shard_map/all_gather | solution.py:17
  228.4 16.6 %fusion.7 = bf16[1024,512]{0,1:T(8,128)(2,1)} fusion(f32[1024,1024]{1,0:T(8,128)} %all-gather.3.cloned.1.call-done, f32[1024,512]{1,0:T(8,128)} %all-reduce.2.cloned.1.call-done), kind=kOutput, calls=%fused_computation.5 | convolution fusion | flops 6443499520 | bytes 7340032 | tf_op jit(solution)/shard_map/dot_general | solution.py:24
  245.0 0.0 all-gather.5.cloned.1.call-update
  245.0 90.7 %all-gather.5.cloned.1.call-done = bf16[1024,4096]{0,1:T(8,128)(2,1)} async-done(((bf16[1024,512]{0,1:T(8,128)(2,1)}), bf16[1024,4096]{0,1:T(8,128)(2,1)}) %all-gather.5.cloned.1.call-update) | async-done | bytes 8388624 | tf_op jit(solution)/shard_map/all_gather | solution.py:25
  335.7 2.6 convolution_multiply_fusion
Async XLA Ops:
  6.5 161.7 %all-reduce.2.cloned.1.call-start = ((), (), s32[]{:S(2)}) async-start(), calls=%async_computation | async-start | bytes 4194304 | tf_op jit(solution)/shard_map/psum | solution.py:23
  20.9 207.5 %all-gather.3.cloned.1.call-start = ((), (), s32[]{:S(2)}) async-start(), calls=%async_computation.1 | async-start | bytes 4456448 | tf_op jit(solution)/shard_map/all_gather | solution.py:17
  21.7 314.1 %all-gather.5.cloned.1.call-start = ((), (), s32[]{:S(2)}) async-start(), calls=%async_computation.2 | async-start | bytes 9437184 | tf_op jit(solution)/shard_map/all_gather | solution.py:25
Sparse Core Ops, SparseCore 0:
  21.0 147.1 all-reduce.1
  170.7 57.6 all-gather.2
  245.1 90.5 all-gather.4
where the time goes:
time: 345 us
  waiting for transfers between devices  298 us (86%)
  matrix products  33.6 us (10%)
  between operations  13.1 us (4%)
    psum x1, waiting for transfers between devices, body(): sketch = lax.psum(partial_value, 'param') * norm_factor  147 us
    all_gather x1, waiting for transfers between devices, body(): all_columns = lax.all_gather(whitened, 'ex', axis=1, tiled=True)  90.7 us
    all_gather x1, waiting for transfers between devices, body(): whole_whitener = lax.all_gather(whitener, 'param', axis=0, tiled=True)  60.1 us
    dot_general x1, matrix products, body(): jnp.dot(whole_whitener, sketch, precision=lax.Precision.HIGHEST)  16.6 us
    dot_general x1, matrix products, body(): lax.dot_general(projection, low_grads, (((0,), (0,)), ((), ())), preferre...  14.3 us
  transfers between devices with their start and end apart: 3, of which 3 were waited for; matrix products, arithmetic and copies ran while one was open for 0% of the time, Pallas kernels for 0%

commit v1 on v0

v1 whole, which is shorter than its diff:
```python
import math

import jax
import jax.numpy as jnp
from jax import lax
from jax.sharding import Mesh, PartitionSpec as P

BF16 = jnp.bfloat16
F32 = jnp.float32
RING = ("x", "y_hi")
COLS = ("y_lo", "z")


def matmul(a, b, dims):
    return lax.dot_general(a, b, (dims, ((), ())), preferred_element_type=F32)


def gather(block, axes):
    n = lax.axis_size(axes)
    copies = jnp.broadcast_to(block[None], (n,) + block.shape)
    return lax.all_to_all(copies, axes, 0, 0, tiled=True)


def body(grads, projection, whitener):
    n = lax.axis_size(RING)
    core = lax.axis_index("core")
    sketch_rows = projection.shape[1]
    norm_factor = 1.0 / math.sqrt(grads.shape[0] * n * lax.axis_size("core"))
    width = grads.shape[1]
    half = width // 2

    whole = lax.all_gather(whitener.astype(BF16), ("x", "y_hi", "core"), axis=0, tiled=True)

    partial = matmul(grads.astype(BF16), projection, ((0,), (0,)))
    keep = lax.dynamic_slice_in_dim(partial, core * half, half, 0)
    give = lax.dynamic_slice_in_dim(partial, (1 - core) * half, half, 0).astype(BF16)
    swap = [(0, 1), (1, 0)]
    chip = keep + lax.ppermute(give, "core", swap).astype(F32)
    blocks = chip.astype(BF16).reshape(n, half // n, sketch_rows)
    pieces = lax.all_to_all(blocks, RING, 0, 0, tiled=True)
    sketch = (jnp.sum(pieces.astype(F32), axis=0) * norm_factor).astype(BF16)
    white = matmul(sketch, whole, ((1,), (1,))).astype(BF16)

    turn = [(q * n + e, e * n + q) for e in range(n) for q in range(n)]
    other = lax.ppermute(white, RING + COLS, turn)
    row_half = gather(white, RING).reshape(half, sketch_rows)
    row_other = lax.ppermute(row_half, "core", swap)
    cols = gather(other, COLS).reshape(half, sketch_rows)
    own = matmul(row_half, cols, ((1,), (1,)))
    far = matmul(row_other, cols, ((1,), (1,)))
    first = jnp.where(core == 0, own, far)
    second = jnp.where(core == 0, far, own)
    return jnp.concatenate([first, second], axis=0) * (1.0 / sketch_rows)


def solution(mesh):
    fine = Mesh(mesh.devices.reshape(4, 2, 2, 2, 4), ("x", "y_hi", "core", "y_lo", "z"))
    param = ("x", "y_hi", "core")
    return jax.shard_map(
        body,
        mesh=fine,
        in_specs=(P(param, COLS), P(param, None), P(param, None)),
        out_specs=P(COLS, param),
        check_vma=False,
    )
```

time: 345 us -> 105 us (0.30)
  waiting for transfers between devices: 298 us -> 40 us
  matrix products: 33.6 us -> 16.3 us
  blocking collectives: 0 us -> 16.5 us
  starting transfers between devices: 0.08 us -> 13 us
    psum x1 -> x0, waiting for transfers between devices: 147 us -> none  [body(): sketch = lax.psum(partial_value, 'param') * norm_factor]
    all_gather x2 -> x1, waiting for transfers between devices: 151 us -> 20.5 us  [body(): lax.all_gather(whitener.astype(BF16), ('x', 'y_hi', 'core'), axis=0, tile...]
    all_to_all x0 -> x2, waiting for transfers between devices: none -> 18 us  [gather(): return lax.all_to_all(copies, axes, 0, 0, tiled=True)]
    dot_general x3 -> x4, matrix products: 33.6 us -> 16.3 us  [matmul(): return lax.dot_general(a, b, (dims, ((), ())), preferred_element_type=F32)]
    all_to_all x0 -> x1, blocking collectives: none -> 16.5 us  [body(): pieces = lax.all_to_all(blocks, RING, 0, 0, tiled=True)]
    all_to_all x0 -> x2, starting transfers between devices: none -> 7.44 us  [gather(): return lax.all_to_all(copies, axes, 0, 0, tiled=True)]
    ppermute x0 -> x3, starting transfers between devices: none -> 5.53 us  [the longest x1 3.37 us: body(): row_other = lax.ppermute(row_half, 'core', swap)]
  transfers between devices with their start and end apart: 3 -> 6, of which waited for: 3 -> 4; matrix products, arithmetic and copies ran while one was open for 0% -> 14% of each run, Pallas kernels for 0% -> 0%
where the time goes in v1:
time: 105 us; the launch traced here: 104 us
  waiting for transfers between devices  40 us (38%)
  blocking collectives  16.5 us (16%)
  matrix products  16.3 us (16%)
  between operations  13.5 us (13%)
  starting transfers between devices  13 us (12%)
  other arithmetic  2.67 us (3%)
  local copies, waits for them, and re-layouts  1.8 us (2%)
    all_gather x1, waiting for transfers between devices, body(): lax.all_gather(whitener.astype(BF16), ('x', 'y_hi', 'core'), axis=0, tile...  20.5 us
    all_to_all x2, waiting for transfers between devices, gather(): return lax.all_to_all(copies, axes, 0, 0, tiled=True)  18 us
    all_to_all x1, blocking collectives, body(): pieces = lax.all_to_all(blocks, RING, 0, 0, tiled=True)  16.5 us
    dot_general x4, matrix products, matmul(): return lax.dot_general(a, b, (dims, ((), ())), preferred_element_type=F32)  16.3 us
    all_to_all x2, starting transfers between devices, gather(): return lax.all_to_all(copies, axes, 0, 0, tiled=True)  7.44 us
    ppermute x1, starting transfers between devices, body(): row_other = lax.ppermute(row_half, 'core', swap)  3.37 us
  transfers between devices with their start and end apart: 6, of which 4 were waited for; matrix products, arithmetic and copies ran while one was open for 14% of the time, Pallas kernels for 0%

profile of v1, /device:TPU:1, one launch (start us, length us, event | category | flops | bytes accessed | tf_op | source)
XLA Modules:
  0.0 103.7 jit_solution(16805927235949984849)
XLA Ops:
  6.5 1.6 %convert_element_type.30 = bf16[64,1024]{1,0:T(8,128)(2,1)} convert(f32[64,1024]{1,0:T(8,128)} %param.5) | non-fusion elementwise | flops 65536 | bytes 393216 | tf_op jit(solution)/shard_map/convert_element_type | solution.py:32
  8.2 0.0 all-gather.2.cloned.1.call-update
  8.2 13.3 %fusion = f32[512,1024]{1,0:T(8,128)S(1)} fusion(bf16[6144,1024]{1,0:T(8,128)(2,1)} %param.4, f32[6144,512]{1,0:T(8,128)} %param.3), kind=kOutput, calls=%fused_computation | convolution fusion | flops 6445596672 | bytes 27262976 | tf_op jit(solution)/shard_map/dot_general | solution.py:15
  21.5 0.1 dynamic-slice_convert_fusion
  21.6 1.5 %collective-permute-start = (bf16[256,1024]{1,0:T(8,128)(2,1)S(1)}, bf16[256,1024]{1,0:T(8,128)(2,1)S(1)}, u32[]{:S(2)}, u32[]{:S(2)}) collective-permute-start(bf16[256,1024]{1,0:T(8,128)(2,1)S(1)} %dynamic-slice_convert_fusion), channel_id=1, source_target_pairs={{0,8},{8,0},{1,9},{9,1},{2,10},{10,2},{3,11},{11,3},{4,12},{12,4},... | collective-permute-start | bytes 1572872 | tf_op jit(solution)/shard_map/ppermute | solution.py:38
  23.1 1.5 %collective-permute-done = bf16[256,1024]{1,0:T(8,128)(2,1)S(1)} collective-permute-done((bf16[256,1024]{1,0:T(8,128)(2,1)S(1)}, bf16[256,1024]{1,0:T(8,128)(2,1)S(1)}, u32[]{:S(2)}, u32[]{:S(2)}) %collective-permute-start) | collective-permute-done | bytes 524320 | tf_op jit(solution)/shard_map/ppermute | solution.py:38
  24.6 0.1 add_convert_fusion
  24.8 16.5 %all_to_all.15 = bf16[8,32,1024]{2,1,0:T(8,128)(2,1)S(1)} all-to-all(bf16[8,32,1024]{2,1,0:T(8,128)(2,1)S(1)} %bitcast.11), channel_id=1, replica_groups=mesh['x'=4,'y_hi'=2,'core'=2,'y_lo'=2,'z'=4] {'x','y_hi'}, dimensions={0} | all-to-all | bytes 1048576 | tf_op jit(solution)/shard_map/all_to_all | solution.py:40
  41.3 0.1 convert_reduce_fusion
  41.3 20.5 %all-gather.2.cloned.1.call-done = bf16[1024,1024]{1,0:T(8,128)(2,1)} async-done(((bf16[64,1024]{1,0:T(8,128)(2,1)}), bf16[1024,1024]{1,0:T(8,128)(2,1)}) %all-gather.2.cloned.1.call-update) | async-done | bytes 2097168 | tf_op jit(solution)/shard_map/all_gather | solution.py:32
  61.8 2.3 %convolution_convert_fusion = bf16[32,1024]{1,0:T(8,128)(2,1)S(1)} fusion(bf16[1024,1024]{1,0:T(8,128)(2,1)} %all-gather.2.cloned.1.call-done, f32[32,1024]{1,0:T(8,128)S(1)} %convert_reduce_fusion), kind=kOutput, calls=%fused_computation.2 | convolution fusion | flops 67207168 | bytes 2293760 | tf_op jit(solution)/shard_map/dot_general | solution.py:15
  64.1 0.9 broadcast_in_dim.4
  65.0 3.5 %all-to-all-start.1 = ((bf16[8,32,1024]{2,1,0:T(8,128)(2,1)}), bf16[8,32,1024]{2,1,0:T(8,128)(2,1)S(1)}, u32[]{:S(2)}, u32[]{:S(2)}) async-start(bf16[8,32,1024]{2,1,0:T(8,128)(2,1)} %broadcast_in_dim.4), calls=%async_computation.1 | async-start | bytes 1048576 | tf_op jit(solution)/shard_map/all_to_all | solution.py:21
  68.5 0.7 collective-permute-start.1
  69.2 10.2 %all-to-all-done.1 = bf16[8,32,1024]{2,1,0:T(8,128)(2,1)S(1)} async-done(((bf16[8,32,1024]{2,1,0:T(8,128)(2,1)}), bf16[8,32,1024]{2,1,0:T(8,128)(2,1)S(1)}, u32[]{:S(2)}, u32[]{:S(2)}) %all-to-all-start.1) | async-done | bytes 524320 | tf_op jit(solution)/shard_map/all_to_all | solution.py:21
  79.4 3.4 %collective-permute-start.2 = (bf16[256,1024]{1,0:T(8,128)(2,1)S(1)}, bf16[256,1024]{1,0:T(8,128)(2,1)S(1)}, u32[]{:S(2)}, u32[]{:S(2)}) collective-permute-start(bf16[256,1024]{1,0:T(8,128)(2,1)S(1)} %bitcast.12), channel_id=1, source_target_pairs={{0,8},{8,0},{1,9},{9,1},{2,10},{10,2},{3,11},{11,3},{4,12},{12,4},... | collective-permute-start | bytes 1572872 | tf_op jit(solution)/shard_map/ppermute | solution.py:47
  82.8 0.0 collective-permute-done.1
  82.8 0.9 broadcast_in_dim.5
  83.6 3.9 %all-to-all-start.2 = ((bf16[8,32,1024]{2,1,0:T(8,128)(2,1)}), bf16[8,32,1024]{2,1,0:T(8,128)(2,1)S(1)}, u32[]{:S(2)}, u32[]{:S(2)}) async-start(bf16[8,32,1024]{2,1,0:T(8,128)(2,1)} %broadcast_in_dim.5), calls=%async_computation.2 | async-start | bytes 1048576 | tf_op jit(solution)/shard_map/all_to_all | solution.py:21
  87.6 7.7 %all-to-all-done.2 = bf16[8,32,1024]{2,1,0:T(8,128)(2,1)S(1)} async-done(((bf16[8,32,1024]{2,1,0:T(8,128)(2,1)}), bf16[8,32,1024]{2,1,0:T(8,128)(2,1)S(1)}, u32[]{:S(2)}, u32[]{:S(2)}) %all-to-all-start.2) | async-done | bytes 524320 | tf_op jit(solution)/shard_map/all_to_all | solution.py:21
  95.3 0.0 collective-permute-done.2
  95.3 0.3 fusion.4
  95.6 0.3 broadcast_select_fusion.1
  96.0 0.8 maximum_multiply_fusion
  (1 shorter events, 0.0 us)
Async XLA Ops:
  6.5 55.3 %all-gather.2.cloned.1.call-start = ((), (), s32[]{:S(2)}) async-start(), calls=%async_computation.3 | async-start | bytes 2228224 | tf_op jit(solution)/shard_map/all_gather | solution.py:32
  21.6 3.0 %collective-permute-start = (bf16[256,1024]{1,0:T(8,128)(2,1)S(1)}, bf16[256,1024]{1,0:T(8,128)(2,1)S(1)}, u32[]{:S(2)}, u32[]{:S(2)}) collective-permute-start(bf16[256,1024]{1,0:T(8,128)(2,1)S(1)} %dynamic-slice_convert_fusion), channel_id=1, source_target_pairs={{0,8},{8,0},{1,9},{9,1},{2,10},{10,2},{3,11},{11,3},{4,12},{12,4},... | collective-permute-start | bytes 1572872 | tf_op jit(solution)/shard_map/ppermute | solution.py:38
  65.0 14.4 %all-to-all-start.1 = ((bf16[8,32,1024]{2,1,0:T(8,128)(2,1)}), bf16[8,32,1024]{2,1,0:T(8,128)(2,1)S(1)}, u32[]{:S(2)}, u32[]{:S(2)}) async-start(bf16[8,32,1024]{2,1,0:T(8,128)(2,1)} %broadcast_in_dim.4), calls=%async_computation.1 | async-start | bytes 1048576 | tf_op jit(solution)/shard_map/all_to_all | solution.py:21
  68.5 14.3 %collective-permute-start.1 = (bf16[32,1024]{1,0:T(8,128)(2,1)S(1)}, bf16[32,1024]{1,0:T(8,128)(2,1)S(1)}, u32[]{:S(2)}, u32[]{:S(2)}) collective-permute-start(bf16[32,1024]{1,0:T(8,128)(2,1)S(1)} %convolution_convert_fusion), channel_id=1, source_target_pairs={{0,0},{16,1},{32,2},{48,3},{64,4},{80,5},{96,6},{112,7},{1,16},{17... | collective-permute-start | bytes 196616 | tf_op jit(solution)/shard_map/ppermute | solution.py:45
  79.4 15.9 %collective-permute-start.2 = (bf16[256,1024]{1,0:T(8,128)(2,1)S(1)}, bf16[256,1024]{1,0:T(8,128)(2,1)S(1)}, u32[]{:S(2)}, u32[]{:S(2)}) collective-permute-start(bf16[256,1024]{1,0:T(8,128)(2,1)S(1)} %bitcast.12), channel_id=1, source_target_pairs={{0,8},{8,0},{1,9},{9,1},{2,10},{10,2},{3,11},{11,3},{4,12},{12,4},... | collective-permute-start | bytes 1572872 | tf_op jit(solution)/shard_map/ppermute | solution.py:47
  83.6 11.7 %all-to-all-start.2 = ((bf16[8,32,1024]{2,1,0:T(8,128)(2,1)}), bf16[8,32,1024]{2,1,0:T(8,128)(2,1)S(1)}, u32[]{:S(2)}, u32[]{:S(2)}) async-start(bf16[8,32,1024]{2,1,0:T(8,128)(2,1)} %broadcast_in_dim.5), calls=%async_computation.2 | async-start | bytes 1048576 | tf_op jit(solution)/shard_map/all_to_all | solution.py:21
Sparse Core Ops, SparseCore 0:
  9.8 52.0 all-gather.1

commit v2 on v1

v2 whole, which is shorter than its diff:
```python
import math

import jax
import jax.numpy as jnp
from jax import lax
from jax.experimental import pallas as pl
from jax.experimental.pallas import tpu as pltpu
from jax.sharding import Mesh, PartitionSpec as P

BF16 = jnp.bfloat16
F32 = jnp.float32
RING = ("x", "y_hi")
COLS = ("y_lo", "z")
SWAP = [(0, 1), (1, 0)]
TILE = 512
STEPS = (1, 2, 3, 3, 2, 1)


def matmul(a, b, dims):
    return lax.dot_general(a, b, (dims, ((), ())), preferred_element_type=F32)


def send_all(copies, axes):
    return lax.all_to_all(copies, axes, 0, 0, tiled=True)


def project_kernel(
    core_ref, grads_hbm, projection_hbm, keep_ref, give_ref, grads_ref, projection_ref, total, sems
):
    rows = grads_ref.shape[0]
    half = keep_ref.shape[1]
    copies = []
    for i in range(rows // TILE):
        part = pl.ds(i * TILE, TILE)
        pair = (
            pltpu.make_async_copy(grads_hbm.at[part], grads_ref.at[part], sems.at[0, i]),
            pltpu.make_async_copy(projection_hbm.at[part], projection_ref.at[part], sems.at[1, i]),
        )
        for copy in pair:
            copy.start()
        copies.append(pair)
    first = 0
    for count in STEPS:
        for pair in copies[first : first + count]:
            for copy in pair:
                copy.wait()
        part = pl.ds(first * TILE, count * TILE)
        term = matmul(grads_ref[part, :].astype(BF16), projection_ref[part, :], ((0,), (0,)))
        if first == 0:
            total[...] = term
        else:
            total[...] += term
        first += count
    mine = pl.multiple_of(core_ref[0] * half, half)
    theirs = pl.multiple_of((1 - core_ref[0]) * half, half)
    keep_ref[...] = total[:, pl.ds(mine, half)]
    give_ref[...] = total[:, pl.ds(theirs, half)].astype(BF16)


def project(core, grads, projection):
    rows, width = grads.shape
    cols = projection.shape[1]
    half = cols // 2
    hbm = pl.BlockSpec(memory_space=pl.ANY)
    vmem = pl.BlockSpec(memory_space=pltpu.VMEM)
    return pl.pallas_call(
        project_kernel,
        out_shape=(
            jax.ShapeDtypeStruct((width, half), F32),
            jax.ShapeDtypeStruct((width, half), BF16),
        ),
        in_specs=[pl.BlockSpec(memory_space=pltpu.SMEM), hbm, hbm],
        out_specs=[vmem, vmem],
        scratch_shapes=[
            pltpu.VMEM((rows, width), grads.dtype),
            pltpu.VMEM((rows, cols), projection.dtype),
            pltpu.VMEM((width, cols), F32),
            pltpu.SemaphoreType.DMA((2, rows // TILE)),
        ],
        compiler_params=pltpu.CompilerParams(vmem_limit_bytes=52 << 20),
        cost_estimate=pl.CostEstimate(
            flops=2 * rows * width * cols,
            bytes_accessed=rows * (4 * width + 2 * cols),
            transcendentals=0,
        ),
        name="project",
    )(core, grads, projection)


def spread_kernel(part_ref, out_ref):
    part = part_ref[...].astype(BF16)
    for i in range(out_ref.shape[0]):
        out_ref[i] = part


def spread(part, count):
    return pl.pallas_call(
        spread_kernel,
        out_shape=jax.ShapeDtypeStruct((count,) + part.shape, BF16),
        in_specs=[pl.BlockSpec(memory_space=pltpu.VMEM)],
        out_specs=pl.BlockSpec(memory_space=pltpu.VMEM),
        name="spread",
    )(part)


def call(kernel, out_shape, flops, *args, scratch=(), name):
    vmem = pl.BlockSpec(memory_space=pltpu.VMEM)
    moved = sum(a.size * a.dtype.itemsize for a in args[1:])
    return pl.pallas_call(
        kernel,
        out_shape=out_shape,
        in_specs=[pl.BlockSpec(memory_space=pltpu.SMEM)] + [vmem] * (len(args) - 1),
        out_specs=jax.tree.map(lambda _: vmem, out_shape),
        scratch_shapes=scratch,
        compiler_params=pltpu.CompilerParams(vmem_limit_bytes=24 << 20),
        cost_estimate=pl.CostEstimate(flops=flops, bytes_accessed=moved, transcendentals=0),
        name=name,
    )(*args)


def reduce_kernel(core_ref, pieces_ref, out_ref, *, groups, scale):
    count, rows, _ = pieces_ref.shape
    for e in range(groups):
        total = pieces_ref[e].astype(F32)
        for q in range(1, count // groups):
            total += pieces_ref[q * groups + e].astype(F32)
        out_ref[e * rows : (e + 1) * rows, :] = total * scale


def whiten_kernel(core_ref, mine_ref, theirs_ref, whitener_ref, out_ref):
    rows, half = mine_ref.shape
    total = jnp.zeros((rows, whitener_ref.shape[0]), F32)
    for ref, side in ((mine_ref, core_ref[0]), (theirs_ref, 1 - core_ref[0])):
        part = ref[...]
        high = part.astype(BF16)
        low = (part - high.astype(F32)).astype(BF16)
        block = whitener_ref[:, pl.ds(pl.multiple_of(side * half, half), half)]
        term = matmul(jnp.concatenate([high, low], axis=0), block, ((1,), (1,)))
        total += term[:rows] + term[rows:]
    white = total.astype(BF16)
    size = out_ref.shape[1] // 2
    n = rows // size
    for q in range(n):
        for e in range(n):
            out_ref[q * n + e, :size, :] = white[e * size : (e + 1) * size]
            out_ref[q * n + e, size:, :] = white[q * size : (q + 1) * size]


def score_kernel(core_ref, pieces_ref, keep_ref, give_ref, rows_ref, cols_ref):
    count, size, _ = pieces_ref.shape
    size //= 2
    for i in range(count):
        rows_ref[i * size : (i + 1) * size, :] = pieces_ref[i, :size, :]
        cols_ref[i * size : (i + 1) * size, :] = pieces_ref[i, size:, :]
    half = keep_ref.shape[1]
    mine = pl.multiple_of(core_ref[0] * half, half)
    theirs = pl.multiple_of((1 - core_ref[0]) * half, half)
    rows = rows_ref[...]
    give_ref[...] = matmul(rows, cols_ref[pl.ds(theirs, half), :], ((1,), (1,))).astype(BF16)
    keep_ref[...] = matmul(rows, cols_ref[pl.ds(mine, half), :], ((1,), (1,)))


def body(grads, projection, whitener):
    n = lax.axis_size(RING)
    chips = RING + COLS
    core = lax.axis_index("core").astype(jnp.int32).reshape(1)
    sketch_rows = projection.shape[1]
    norm_factor = 1.0 / math.sqrt(grads.shape[0] * n * lax.axis_size("core"))
    width = grads.shape[1]
    half = sketch_rows // 2
    size = width // (n * n)

    own = send_all(spread(whitener, n), RING).reshape(half, sketch_rows)

    keep, give = project(core, grads, projection)
    got = lax.ppermute(give, "core", SWAP)
    got, own = lax.optimization_barrier((got, own))
    blocks = (keep + got.astype(F32)).astype(BF16)
    pieces = send_all(blocks.reshape(n * n, size, half), chips)
    shape = jax.ShapeDtypeStruct((n * size, half), F32)
    mine = call(
        lambda *refs: reduce_kernel(*refs, groups=n, scale=norm_factor),
        shape, 0, core, pieces, name="reduce",
    )
    theirs = lax.ppermute(mine, "core", SWAP)
    shape = jax.ShapeDtypeStruct((n * n, 2 * size, half), BF16)
    flops = 4 * n * size * sketch_rows * half
    copies = call(whiten_kernel, shape, flops, core, mine, theirs, own, name="whiten")
    pieces = send_all(copies, chips)
    side = lax.axis_size("core")
    shapes = (
        jax.ShapeDtypeStruct((width, width // side), F32),
        jax.ShapeDtypeStruct((width, width // side), BF16),
    )
    flops = 2 * width * width * half
    scratch = [pltpu.VMEM((width, half), BF16)] * 2
    keep, give = call(score_kernel, shapes, flops, core, pieces, scratch=scratch, name="score")
    got = lax.ppermute(give, "core", SWAP)
    return (keep + got.astype(F32)) * (1.0 / sketch_rows)


def solution(mesh):
    fine = Mesh(mesh.devices.reshape(4, 2, 2, 2, 4), ("x", "y_hi", "core", "y_lo", "z"))
    param = ("x", "y_hi", "core")
    return jax.shard_map(
        body,
        mesh=fine,
        in_specs=(P(param, COLS), P(param, None), P(param, None)),
        out_specs=P(COLS, param),
        check_vma=False,
    )
```

time: 105 us -> 76.3 us (0.73); the launches traced: 104 us -> 76.1 us
  waiting for transfers between devices: 40 us -> 6.21 us
  blocking collectives: 16.5 us -> 41.5 us
  matrix products: 16.3 us -> 0 us
  Pallas kernels: 0 us -> 13.5 us
  between operations: 13.5 us -> 0.04 us
  local copies, waits for them, and re-layouts: 1.8 us -> 0 us
  other arithmetic: 2.67 us -> 1.01 us
    all_to_all x1 -> x2, blocking collectives: 16.5 us -> 41.5 us  [send_all(): return lax.all_to_all(copies, axes, 0, 0, tiled=True)]
    all_gather x1 -> x0, waiting for transfers between devices: 20.5 us -> none  [body(): lax.all_gather(whitener.astype(BF16), ('x', 'y_hi', 'core'), axis=0, tile...]
    dot_general x4 -> x0, matrix products: 16.3 us -> none  [matmul(): return lax.dot_general(a, b, (dims, ((), ())), preferred_element_type=F32)]
    all_to_all x2 -> x1, waiting for transfers between devices: 18 us -> 2.53 us  [send_all(): return lax.all_to_all(copies, axes, 0, 0, tiled=True)]
    pallas_call x0 -> x5, Pallas kernels: none -> 13.5 us  [the longest x1 10.4 us: project(): pl.pallas_call(project_kernel, out_shape=(jax.ShapeDtypeStruct((width, ha...]
    ppermute x3, waiting for transfers between devices: 1.54 us -> 3.69 us  [the longest x2 2.7 us: body(): got = lax.ppermute(give, 'core', SWAP)]
    convert_element_type x2 -> x0, other arithmetic: 1.76 us -> none  [the longest x1 1.62 us: body(): whitener.astype(BF16)]
    broadcast_in_dim x2 -> x0, local copies, waits for them, and re-layouts: 1.72 us -> none  [gather(): copies = jnp.broadcast_to(block[None], (n,) + block.shape)]
  transfers between devices with their start and end apart: 6 -> 4, of which waited for: 4 -> 4; matrix products, arithmetic and copies ran while one was open for 14% -> 0% of each run, Pallas kernels for 0% -> 14%
where the time goes in v2:
time: 76.3 us; the launch traced here: 76.1 us
  blocking collectives  41.5 us (54%)
  starting transfers between devices  13.8 us (18%)
  Pallas kernels  13.5 us (18%)
  waiting for transfers between devices  6.21 us (8%)
  other arithmetic  1.01 us (1%)
    all_to_all x2, blocking collectives, send_all(): return lax.all_to_all(copies, axes, 0, 0, tiled=True)  41.5 us
    pallas_call x1, Pallas kernels, project(): pl.pallas_call(project_kernel, out_shape=(jax.ShapeDtypeStruct((width, ha...  10.4 us
    all_to_all x1, starting transfers between devices, send_all(): return lax.all_to_all(copies, axes, 0, 0, tiled=True)  7.48 us
    ppermute x2, starting transfers between devices, body(): got = lax.ppermute(give, 'core', SWAP)  3.75 us
    ppermute x2, waiting for transfers between devices, body(): got = lax.ppermute(give, 'core', SWAP)  2.7 us
    ppermute x1, starting transfers between devices, body(): theirs = lax.ppermute(mine, 'core', SWAP)  2.58 us
    all_to_all x1, waiting for transfers between devices, send_all(): return lax.all_to_all(copies, axes, 0, 0, tiled=True)  2.53 us
    pallas_call x1, Pallas kernels, spread(): pl.pallas_call(spread_kernel, out_shape=jax.ShapeDtypeStruct((count,) + p...  1.99 us
  transfers between devices with their start and end apart: 4, of which 4 were waited for; matrix products, arithmetic and copies ran while one was open for 0% of the time, Pallas kernels for 14%

profile of v2, /device:TPU:1, one launch (start us, length us, event | category | flops | bytes accessed | tf_op | source)
XLA Modules:
  0.0 76.1 jit_solution(11483464222906215988)
XLA Ops:
  0.0 2.0 %spread.1 = bf16[8,64,1024]{2,1,0:T(8,128)(2,1)} custom-call(f32[64,1024]{1,0:T(8,128)} %part_ref.1), custom_call_target="tpu_custom_call" | custom-call | tf_op jit(solution)/shard_map/spread/pallas_call | solution.py:97
  2.0 7.5 %all-to-all-start = ((bf16[8,64,1024]{2,1,0:T(8,128)(2,1)}), bf16[8,64,1024]{2,1,0:T(8,128)(2,1)S(1)}, u32[]{:S(2)}, u32[]{:S(2)}) async-start(bf16[8,64,1024]{2,1,0:T(8,128)(2,1)} %spread.1), calls=%async_computation | async-start | bytes 2097152 | tf_op jit(solution)/shard_map/all_to_all | solution.py:24
  9.5 10.4 %project.1 = (f32[512,512]{1,0:T(8,128)S(1)}, bf16[512,512]{1,0:T(8,128)(2,1)S(1)}) custom-call(s32[1]{0:T(128)} %bitcast.core_ref.refs_0_, f32[6144,512]{1,0:T(8,128)} %grads_hbm.1, bf16[6144,1024]{1,0:T(8,128)(2,1)} %projection_hbm.1), custom_call_target="tpu_custom_call" | custom-call | flops 6442450944 | bytes 25165824 | tf_op jit(solution)/shard_map/project/pallas_call | solution.py:66
  19.9 1.0 %collective-permute-start = (bf16[512,512]{1,0:T(8,128)(2,1)S(1)}, bf16[512,512]{1,0:T(8,128)(2,1)S(1)}, u32[]{:S(2)}, u32[]{:S(2)}) collective-permute-start(bf16[512,512]{1,0:T(8,128)(2,1)S(1)} %get-tuple-element.12), channel_id=1, source_target_pairs={{0,8},{8,0},{1,9},{9,1},{2,10},{10,2},{3,11},{11,3},{4,12},{12,4},... | collective-permute-start | bytes 1572872 | tf_op jit(solution)/shard_map/ppermute | solution.py:176
  20.9 1.5 %collective-permute-done = bf16[512,512]{1,0:T(8,128)(2,1)S(1)} collective-permute-done((bf16[512,512]{1,0:T(8,128)(2,1)S(1)}, bf16[512,512]{1,0:T(8,128)(2,1)S(1)}, u32[]{:S(2)}, u32[]{:S(2)}) %collective-permute-start) | collective-permute-done | bytes 524320 | tf_op jit(solution)/shard_map/ppermute | solution.py:176
  22.4 2.5 %all-to-all-done = bf16[8,64,1024]{2,1,0:T(8,128)(2,1)S(1)} async-done(((bf16[8,64,1024]{2,1,0:T(8,128)(2,1)}), bf16[8,64,1024]{2,1,0:T(8,128)(2,1)S(1)}, u32[]{:S(2)}, u32[]{:S(2)}) %all-to-all-start) | async-done | bytes 1048608 | tf_op jit(solution)/shard_map/all_to_all | solution.py:24
  25.0 0.2 fusion
  25.1 20.2 %all_to_all.15.refs_1_ = bf16[64,8,512]{2,1,0:T(8,128)(2,1)S(1)} all-to-all(bf16[64,8,512]{2,1,0:T(8,128)(2,1)S(1)} %fusion), channel_id=1, replica_groups=mesh['x'=4,'y_hi'=2,'core'=2,'y_lo'=2,'z'=4] {'x','y_hi','y_lo','z'}, dimensions={0} | all-to-all | bytes 1048576 | tf_op jit(solution)/shard_map/all_to_all | solution.py:24
  45.4 0.1 reduce.1.mine_ref
  45.4 2.6 %collective-permute-start.1 = (f32[64,512]{1,0:T(8,128)S(1)}, f32[64,512]{1,0:T(8,128)S(1)}, u32[]{:S(2)}, u32[]{:S(2)}) collective-permute-start(f32[64,512]{1,0:T(8,128)S(1)} %reduce.1.mine_ref), channel_id=1, source_target_pairs={{0,8},{8,0},{1,9},{9,1},{2,10},{10,2},{3,11},{11,3},{4,12},{12,4},... | collective-permute-start | bytes 393224 | tf_op jit(solution)/shard_map/ppermute | solution.py:185
  48.0 1.0 %collective-permute-done.1.theirs_ref = f32[64,512]{1,0:T(8,128)S(1)} collective-permute-done((f32[64,512]{1,0:T(8,128)S(1)}, f32[64,512]{1,0:T(8,128)S(1)}, u32[]{:S(2)}, u32[]{:S(2)}) %collective-permute-start.1) | collective-permute-done | bytes 131104 | tf_op jit(solution)/shard_map/ppermute | solution.py:185
  49.0 0.5 whiten.1
  49.5 21.3 %all_to_all.16.pieces_ref = bf16[64,16,512]{2,1,0:T(8,128)(2,1)S(1)} all-to-all(bf16[64,16,512]{2,1,0:T(8,128)(2,1)S(1)} %whiten.1), channel_id=1, replica_groups=mesh['x'=4,'y_hi'=2,'core'=2,'y_lo'=2,'z'=4] {'x','y_hi','y_lo','z'}, dimensions={0} | all-to-all | bytes 2097152 | tf_op jit(solution)/shard_map/all_to_all | solution.py:24
  70.8 0.5 score.1
  71.3 2.7 %collective-permute-start.2 = (bf16[512,256]{1,0:T(8,128)(2,1)S(1)}, bf16[512,256]{1,0:T(8,128)(2,1)S(1)}, u32[]{:S(2)}, u32[]{:S(2)}) collective-permute-start(bf16[512,256]{1,0:T(8,128)(2,1)S(1)} %get-tuple-element.16), channel_id=1, source_target_pairs={{0,8},{8,0},{1,9},{9,1},{2,10},{10,2},{3,11},{11,3},{4,12},{12,4},... | collective-permute-start | bytes 786440 | tf_op jit(solution)/shard_map/ppermute | solution.py:198
  74.1 1.2 %collective-permute-done.2 = bf16[512,256]{1,0:T(8,128)(2,1)S(1)} collective-permute-done((bf16[512,256]{1,0:T(8,128)(2,1)S(1)}, bf16[512,256]{1,0:T(8,128)(2,1)S(1)}, u32[]{:S(2)}, u32[]{:S(2)}) %collective-permute-start.2) | collective-permute-done | bytes 262176 | tf_op jit(solution)/shard_map/ppermute | solution.py:198
  75.2 0.8 %add_multiply_fusion = f32[512,256]{1,0:T(8,128)} fusion(f32[512,256]{1,0:T(8,128)S(1)} %get-tuple-element.15, bf16[512,256]{1,0:T(8,128)(2,1)S(1)} %collective-permute-done.2), kind=kLoop, calls=%fused_computation.2 | loop fusion | flops 393216 | bytes 1310720 | tf_op jit(solution)/shard_map/mul | solution.py:199
Async XLA Ops:
  2.0 23.0 %all-to-all-start = ((bf16[8,64,1024]{2,1,0:T(8,128)(2,1)}), bf16[8,64,1024]{2,1,0:T(8,128)(2,1)S(1)}, u32[]{:S(2)}, u32[]{:S(2)}) async-start(bf16[8,64,1024]{2,1,0:T(8,128)(2,1)} %spread.1), calls=%async_computation | async-start | bytes 2097152 | tf_op jit(solution)/shard_map/all_to_all | solution.py:24
  19.9 2.6 %collective-permute-start = (bf16[512,512]{1,0:T(8,128)(2,1)S(1)}, bf16[512,512]{1,0:T(8,128)(2,1)S(1)}, u32[]{:S(2)}, u32[]{:S(2)}) collective-permute-start(bf16[512,512]{1,0:T(8,128)(2,1)S(1)} %get-tuple-element.12), channel_id=1, source_target_pairs={{0,8},{8,0},{1,9},{9,1},{2,10},{10,2},{3,11},{11,3},{4,12},{12,4},... | collective-permute-start | bytes 1572872 | tf_op jit(solution)/shard_map/ppermute | solution.py:176
  45.4 3.6 %collective-permute-start.1 = (f32[64,512]{1,0:T(8,128)S(1)}, f32[64,512]{1,0:T(8,128)S(1)}, u32[]{:S(2)}, u32[]{:S(2)}) collective-permute-start(f32[64,512]{1,0:T(8,128)S(1)} %reduce.1.mine_ref), channel_id=1, source_target_pairs={{0,8},{8,0},{1,9},{9,1},{2,10},{10,2},{3,11},{11,3},{4,12},{12,4},... | collective-permute-start | bytes 393224 | tf_op jit(solution)/shard_map/ppermute | solution.py:185
  71.3 3.9 %collective-permute-start.2 = (bf16[512,256]{1,0:T(8,128)(2,1)S(1)}, bf16[512,256]{1,0:T(8,128)(2,1)S(1)}, u32[]{:S(2)}, u32[]{:S(2)}) collective-permute-start(bf16[512,256]{1,0:T(8,128)(2,1)S(1)} %get-tuple-element.16), channel_id=1, source_target_pairs={{0,8},{8,0},{1,9},{9,1},{2,10},{10,2},{3,11},{11,3},{4,12},{12,4},... | collective-permute-start | bytes 786440 | tf_op jit(solution)/shard_map/ppermute | solution.py:198

commit v3 on v2

--- a/solution.py
+++ b/solution.py
@@ -29,6 +29,8 @@
 ):
     rows = grads_ref.shape[0]
     half = keep_ref.shape[1]
+    mine = pl.ds(pl.multiple_of(core_ref[0] * half, half), half)
+    theirs = pl.ds(pl.multiple_of((1 - core_ref[0]) * half, half), half)
     copies = []
     for i in range(rows // TILE):
         part = pl.ds(i * TILE, TILE)
@@ -45,16 +47,19 @@
             for copy in pair:
                 copy.wait()
         part = pl.ds(first * TILE, count * TILE)
-        term = matmul(grads_ref[part, :].astype(BF16), projection_ref[part, :], ((0,), (0,)))
-        if first == 0:
-            total[...] = term
+        grads = grads_ref[part, :].astype(BF16)
+        near = matmul(grads, projection_ref[part, mine], ((0,), (0,)))
+        far = matmul(grads, projection_ref[part, theirs], ((0,), (0,)))
+        first += count
+        if first == count:
+            keep_ref[...] = near
+            total[...] = far
+        elif first < rows // TILE:
+            keep_ref[...] += near
+            total[...] += far
         else:
-            total[...] += term
-        first += count
-    mine = pl.multiple_of(core_ref[0] * half, half)
-    theirs = pl.multiple_of((1 - core_ref[0]) * half, half)
-    keep_ref[...] = total[:, pl.ds(mine, half)]
-    give_ref[...] = total[:, pl.ds(theirs, half)].astype(BF16)
+            keep_ref[...] += near
+            give_ref[...] = (total[...] + far).astype(BF16)
 
 
 def project(core, grads, projection):
@@ -74,7 +79,7 @@
         scratch_shapes=[
             pltpu.VMEM((rows, width), grads.dtype),
             pltpu.VMEM((rows, cols), projection.dtype),
-            pltpu.VMEM((width, cols), F32),
+            pltpu.VMEM((width, half), F32),
             pltpu.SemaphoreType.DMA((2, rows // TILE)),
         ],
         compiler_params=pltpu.CompilerParams(vmem_limit_bytes=52 << 20),
@@ -127,17 +132,24 @@
         out_ref[e * rows : (e + 1) * rows, :] = total * scale
 
 
-def whiten_kernel(core_ref, mine_ref, theirs_ref, whitener_ref, out_ref):
-    rows, half = mine_ref.shape
-    total = jnp.zeros((rows, whitener_ref.shape[0]), F32)
-    for ref, side in ((mine_ref, core_ref[0]), (theirs_ref, 1 - core_ref[0])):
-        part = ref[...]
-        high = part.astype(BF16)
-        low = (part - high.astype(F32)).astype(BF16)
-        block = whitener_ref[:, pl.ds(pl.multiple_of(side * half, half), half)]
-        term = matmul(jnp.concatenate([high, low], axis=0), block, ((1,), (1,)))
-        total += term[:rows] + term[rows:]
-    white = total.astype(BF16)
+def whiten_half(part, block):
+    rows = part.shape[0]
+    high = part.astype(BF16)
+    low = (part - high.astype(F32)).astype(BF16)
+    term = matmul(jnp.concatenate([high, low], axis=0), block, ((1,), (1,)))
+    return term[:rows] + term[rows:]
+
+
+def first_half_kernel(core_ref, mine_ref, whitener_ref, out_ref):
+    half = mine_ref.shape[1]
+    mine = pl.ds(pl.multiple_of(core_ref[0] * half, half), half)
+    out_ref[...] = whiten_half(mine_ref[...], whitener_ref[:, mine])
+
+
+def whiten_kernel(core_ref, first_ref, theirs_ref, whitener_ref, out_ref):
+    rows, half = theirs_ref.shape
+    theirs = pl.ds(pl.multiple_of((1 - core_ref[0]) * half, half), half)
+    white = (first_ref[...] + whiten_half(theirs_ref[...], whitener_ref[:, theirs])).astype(BF16)
     size = out_ref.shape[1] // 2
     n = rows // size
     for q in range(n):
@@ -146,18 +158,21 @@
             out_ref[q * n + e, size:, :] = white[q * size : (q + 1) * size]
 
 
-def score_kernel(core_ref, pieces_ref, keep_ref, give_ref, rows_ref, cols_ref):
+def give_kernel(core_ref, pieces_ref, give_ref, rows_ref, cols_ref):
     count, size, _ = pieces_ref.shape
     size //= 2
     for i in range(count):
         rows_ref[i * size : (i + 1) * size, :] = pieces_ref[i, :size, :]
         cols_ref[i * size : (i + 1) * size, :] = pieces_ref[i, size:, :]
+    half = give_ref.shape[1]
+    theirs = pl.ds(pl.multiple_of((1 - core_ref[0]) * half, half), half)
+    give_ref[...] = matmul(rows_ref[...], cols_ref[theirs, :], ((1,), (1,))).astype(BF16)
+
+
+def keep_kernel(core_ref, rows_ref, cols_ref, keep_ref):
     half = keep_ref.shape[1]
-    mine = pl.multiple_of(core_ref[0] * half, half)
-    theirs = pl.multiple_of((1 - core_ref[0]) * half, half)
-    rows = rows_ref[...]
-    give_ref[...] = matmul(rows, cols_ref[pl.ds(theirs, half), :], ((1,), (1,))).astype(BF16)
-    keep_ref[...] = matmul(rows, cols_ref[pl.ds(mine, half), :], ((1,), (1,)))
+    mine = pl.ds(pl.multiple_of(core_ref[0] * half, half), half)
+    keep_ref[...] = matmul(rows_ref[...], cols_ref[mine, :], ((1,), (1,)))
 
 
 def body(grads, projection, whitener):
@@ -183,19 +198,23 @@
         shape, 0, core, pieces, name="reduce",
     )
     theirs = lax.ppermute(mine, "core", SWAP)
+    flops = 4 * n * size * half * half
+    shape = jax.ShapeDtypeStruct((n * size, half), F32)
+    first = call(first_half_kernel, shape, flops, core, mine, own, name="first_half")
     shape = jax.ShapeDtypeStruct((n * n, 2 * size, half), BF16)
-    flops = 4 * n * size * sketch_rows * half
-    copies = call(whiten_kernel, shape, flops, core, mine, theirs, own, name="whiten")
+    copies = call(whiten_kernel, shape, flops, core, first, theirs, own, name="whiten")
     pieces = send_all(copies, chips)
-    side = lax.axis_size("core")
+    across = width // lax.axis_size("core")
+    flops = 2 * width * across * half
     shapes = (
-        jax.ShapeDtypeStruct((width, width // side), F32),
-        jax.ShapeDtypeStruct((width, width // side), BF16),
+        jax.ShapeDtypeStruct((width, across), BF16),
+        jax.ShapeDtypeStruct((width, half), BF16),
+        jax.ShapeDtypeStruct((width, half), BF16),
     )
-    flops = 2 * width * width * half
-    scratch = [pltpu.VMEM((width, half), BF16)] * 2
-    keep, give = call(score_kernel, shapes, flops, core, pieces, scratch=scratch, name="score")
+    give, rows, cols = call(give_kernel, shapes, flops, core, pieces, name="give")
     got = lax.ppermute(give, "core", SWAP)
+    shape = jax.ShapeDtypeStruct((width, across), F32)
+    keep = call(keep_kernel, shape, flops, core, rows, cols, name="keep")
     return (keep + got.astype(F32)) * (1.0 / sketch_rows)
 
 

time: 76.3 us -> 75.9 us (level)
  no operation moved by 1% of the time
where the time goes in v3:
time: 75.9 us; the launch traced here: 75.7 us
  blocking collectives  41.4 us (55%)
  Pallas kernels  13.8 us (18%)
  starting transfers between devices  13.8 us (18%)
  waiting for transfers between devices  5.68 us (7%)
  other arithmetic  1.01 us (1%)
    all_to_all x2, blocking collectives, send_all(): return lax.all_to_all(copies, axes, 0, 0, tiled=True)  41.4 us
    pallas_call x1, Pallas kernels, project(): pl.pallas_call(project_kernel, out_shape=(jax.ShapeDtypeStruct((width, ha...  10.3 us
    all_to_all x1, starting transfers between devices, send_all(): return lax.all_to_all(copies, axes, 0, 0, tiled=True)  7.48 us
    ppermute x2, starting transfers between devices, body(): got = lax.ppermute(give, 'core', SWAP)  3.69 us
    all_to_all x1, waiting for transfers between devices, send_all(): return lax.all_to_all(copies, axes, 0, 0, tiled=True)  2.64 us
    ppermute x1, starting transfers between devices, body(): theirs = lax.ppermute(mine, 'core', SWAP)  2.6 us
    ppermute x2, waiting for transfers between devices, body(): got = lax.ppermute(give, 'core', SWAP)  2.37 us
    pallas_call x1, Pallas kernels, spread(): pl.pallas_call(spread_kernel, out_shape=jax.ShapeDtypeStruct((count,) + p...  1.99 us
  transfers between devices with their start and end apart: 4, of which 4 were waited for; matrix products, arithmetic and copies ran while one was open for 0% of the time, Pallas kernels for 14%

profile of v3, /device:TPU:1, one launch (start us, length us, event | category | flops | bytes accessed | tf_op | source)
XLA Modules:
  0.0 75.7 jit_solution(479410000630475194)
XLA Ops:
  0.0 2.0 %spread.1 = bf16[8,64,1024]{2,1,0:T(8,128)(2,1)} custom-call(f32[64,1024]{1,0:T(8,128)} %part_ref.1), custom_call_target="tpu_custom_call" | custom-call | tf_op jit(solution)/shard_map/spread/pallas_call | solution.py:102
  2.0 7.5 %all-to-all-start = ((bf16[8,64,1024]{2,1,0:T(8,128)(2,1)}), bf16[8,64,1024]{2,1,0:T(8,128)(2,1)S(1)}, u32[]{:S(2)}, u32[]{:S(2)}) async-start(bf16[8,64,1024]{2,1,0:T(8,128)(2,1)} %spread.1), calls=%async_computation | async-start | bytes 2097152 | tf_op jit(solution)/shard_map/all_to_all | solution.py:24
  9.5 10.3 %project.1 = (f32[512,512]{1,0:T(8,128)S(1)}, bf16[512,512]{1,0:T(8,128)(2,1)S(1)}) custom-call(s32[1]{0:T(128)} %bitcast.core_ref.refs_0_, f32[6144,512]{1,0:T(8,128)} %grads_hbm.1, bf16[6144,1024]{1,0:T(8,128)(2,1)} %projection_hbm.1), custom_call_target="tpu_custom_call" | custom-call | flops 6442450944 | bytes 25165824 | tf_op jit(solution)/shard_map/project/pallas_call | solution.py:71
  19.8 1.0 %collective-permute-start = (bf16[512,512]{1,0:T(8,128)(2,1)S(1)}, bf16[512,512]{1,0:T(8,128)(2,1)S(1)}, u32[]{:S(2)}, u32[]{:S(2)}) collective-permute-start(bf16[512,512]{1,0:T(8,128)(2,1)S(1)} %get-tuple-element.13), channel_id=1, source_target_pairs={{0,8},{8,0},{1,9},{9,1},{2,10},{10,2},{3,11},{11,3},{4,12},{12,4},... | collective-permute-start | bytes 1572872 | tf_op jit(solution)/shard_map/ppermute | solution.py:191
  20.8 1.5 %collective-permute-done = bf16[512,512]{1,0:T(8,128)(2,1)S(1)} collective-permute-done((bf16[512,512]{1,0:T(8,128)(2,1)S(1)}, bf16[512,512]{1,0:T(8,128)(2,1)S(1)}, u32[]{:S(2)}, u32[]{:S(2)}) %collective-permute-start) | collective-permute-done | bytes 524320 | tf_op jit(solution)/shard_map/ppermute | solution.py:191
  22.3 2.6 %all-to-all-done = bf16[8,64,1024]{2,1,0:T(8,128)(2,1)S(1)} async-done(((bf16[8,64,1024]{2,1,0:T(8,128)(2,1)}), bf16[8,64,1024]{2,1,0:T(8,128)(2,1)S(1)}, u32[]{:S(2)}, u32[]{:S(2)}) %all-to-all-start) | async-done | bytes 1048608 | tf_op jit(solution)/shard_map/all_to_all | solution.py:24
  25.0 0.2 fusion
  25.1 20.1 %all_to_all.15.refs_1_ = bf16[64,8,512]{2,1,0:T(8,128)(2,1)S(1)} all-to-all(bf16[64,8,512]{2,1,0:T(8,128)(2,1)S(1)} %fusion), channel_id=1, replica_groups=mesh['x'=4,'y_hi'=2,'core'=2,'y_lo'=2,'z'=4] {'x','y_hi','y_lo','z'}, dimensions={0} | all-to-all | bytes 1048576 | tf_op jit(solution)/shard_map/all_to_all | solution.py:24
  45.2 0.1 reduce.1.mine_ref
  45.3 2.6 %collective-permute-start.1 = (f32[64,512]{1,0:T(8,128)S(1)}, f32[64,512]{1,0:T(8,128)S(1)}, u32[]{:S(2)}, u32[]{:S(2)}) collective-permute-start(f32[64,512]{1,0:T(8,128)S(1)} %reduce.1.mine_ref), channel_id=1, source_target_pairs={{0,8},{8,0},{1,9},{9,1},{2,10},{10,2},{3,11},{11,3},{4,12},{12,4},... | collective-permute-start | bytes 393224 | tf_op jit(solution)/shard_map/ppermute | solution.py:200
  47.9 0.3 first_half.1.first_ref
  48.2 0.7 collective-permute-done.1.theirs_ref
  48.9 0.4 whiten.1
  49.3 21.3 %all_to_all.16.pieces_ref = bf16[64,16,512]{2,1,0:T(8,128)(2,1)S(1)} all-to-all(bf16[64,16,512]{2,1,0:T(8,128)(2,1)S(1)} %whiten.1), channel_id=1, replica_groups=mesh['x'=4,'y_hi'=2,'core'=2,'y_lo'=2,'z'=4] {'x','y_hi','y_lo','z'}, dimensions={0} | all-to-all | bytes 2097152 | tf_op jit(solution)/shard_map/all_to_all | solution.py:24
  70.6 0.4 give.1
  70.9 2.7 %collective-permute-start.2 = (bf16[512,256]{1,0:T(8,128)(2,1)S(1)}, bf16[512,256]{1,0:T(8,128)(2,1)S(1)}, u32[]{:S(2)}, u32[]{:S(2)}) collective-permute-start(bf16[512,256]{1,0:T(8,128)(2,1)S(1)} %get-tuple-element.18), channel_id=1, source_target_pairs={{0,8},{8,0},{1,9},{9,1},{2,10},{10,2},{3,11},{11,3},{4,12},{12,4},... | collective-permute-start | bytes 786440 | tf_op jit(solution)/shard_map/ppermute | solution.py:215
  73.6 0.3 keep.1
  74.0 0.8 %collective-permute-done.2 = bf16[512,256]{1,0:T(8,128)(2,1)S(1)} collective-permute-done((bf16[512,256]{1,0:T(8,128)(2,1)S(1)}, bf16[512,256]{1,0:T(8,128)(2,1)S(1)}, u32[]{:S(2)}, u32[]{:S(2)}) %collective-permute-start.2) | collective-permute-done | bytes 262176 | tf_op jit(solution)/shard_map/ppermute | solution.py:215
  74.8 0.8 %add_multiply_fusion = f32[512,256]{1,0:T(8,128)} fusion(f32[512,256]{1,0:T(8,128)S(1)} %keep.1, bf16[512,256]{1,0:T(8,128)(2,1)S(1)} %collective-permute-done.2), kind=kLoop, calls=%fused_computation.2 | loop fusion | flops 393216 | bytes 1310720 | tf_op jit(solution)/shard_map/mul | solution.py:218
Async XLA Ops:
  2.0 23.0 %all-to-all-start = ((bf16[8,64,1024]{2,1,0:T(8,128)(2,1)}), bf16[8,64,1024]{2,1,0:T(8,128)(2,1)S(1)}, u32[]{:S(2)}, u32[]{:S(2)}) async-start(bf16[8,64,1024]{2,1,0:T(8,128)(2,1)} %spread.1), calls=%async_computation | async-start | bytes 2097152 | tf_op jit(solution)/shard_map/all_to_all | solution.py:24
  19.8 2.5 %collective-permute-start = (bf16[512,512]{1,0:T(8,128)(2,1)S(1)}, bf16[512,512]{1,0:T(8,128)(2,1)S(1)}, u32[]{:S(2)}, u32[]{:S(2)}) collective-permute-start(bf16[512,512]{1,0:T(8,128)(2,1)S(1)} %get-tuple-element.13), channel_id=1, source_target_pairs={{0,8},{8,0},{1,9},{9,1},{2,10},{10,2},{3,11},{11,3},{4,12},{12,4},... | collective-permute-start | bytes 1572872 | tf_op jit(solution)/shard_map/ppermute | solution.py:191
  45.3 3.6 %collective-permute-start.1 = (f32[64,512]{1,0:T(8,128)S(1)}, f32[64,512]{1,0:T(8,128)S(1)}, u32[]{:S(2)}, u32[]{:S(2)}) collective-permute-start(f32[64,512]{1,0:T(8,128)S(1)} %reduce.1.mine_ref), channel_id=1, source_target_pairs={{0,8},{8,0},{1,9},{9,1},{2,10},{10,2},{3,11},{11,3},{4,12},{12,4},... | collective-permute-start | bytes 393224 | tf_op jit(solution)/shard_map/ppermute | solution.py:200
  70.9 3.9 %collective-permute-start.2 = (bf16[512,256]{1,0:T(8,128)(2,1)S(1)}, bf16[512,256]{1,0:T(8,128)(2,1)S(1)}, u32[]{:S(2)}, u32[]{:S(2)}) collective-permute-start(bf16[512,256]{1,0:T(8,128)(2,1)S(1)} %get-tuple-element.18), channel_id=1, source_target_pairs={{0,8},{8,0},{1,9},{9,1},{2,10},{10,2},{3,11},{11,3},{4,12},{12,4},... | collective-permute-start | bytes 786440 | tf_op jit(solution)/shard_map/ppermute | solution.py:215

commit v4 on v3

--- a/solution.py
+++ b/solution.py
@@ -146,7 +146,7 @@
     out_ref[...] = whiten_half(mine_ref[...], whitener_ref[:, mine])
 
 
-def whiten_kernel(core_ref, first_ref, theirs_ref, whitener_ref, out_ref):
+def whiten_kernel(core_ref, first_ref, theirs_ref, whitener_ref, out_ref, *, places):
     rows, half = theirs_ref.shape
     theirs = pl.ds(pl.multiple_of((1 - core_ref[0]) * half, half), half)
     white = (first_ref[...] + whiten_half(theirs_ref[...], whitener_ref[:, theirs])).astype(BF16)
@@ -154,16 +154,17 @@
     n = rows // size
     for q in range(n):
         for e in range(n):
-            out_ref[q * n + e, :size, :] = white[e * size : (e + 1) * size]
-            out_ref[q * n + e, size:, :] = white[q * size : (q + 1) * size]
-
-
-def give_kernel(core_ref, pieces_ref, give_ref, rows_ref, cols_ref):
+            out_ref[places[q][e], :size, :] = white[e * size : (e + 1) * size]
+            out_ref[places[q][e], size:, :] = white[q * size : (q + 1) * size]
+
+
+def give_kernel(core_ref, pieces_ref, give_ref, rows_ref, cols_ref, *, places):
     count, size, _ = pieces_ref.shape
     size //= 2
-    for i in range(count):
-        rows_ref[i * size : (i + 1) * size, :] = pieces_ref[i, :size, :]
-        cols_ref[i * size : (i + 1) * size, :] = pieces_ref[i, size:, :]
+    order = [place for line in places for place in line]
+    for i, place in enumerate(order):
+        rows_ref[i * size : (i + 1) * size, :] = pieces_ref[place, :size, :]
+        cols_ref[i * size : (i + 1) * size, :] = pieces_ref[place, size:, :]
     half = give_ref.shape[1]
     theirs = pl.ds(pl.multiple_of((1 - core_ref[0]) * half, half), half)
     give_ref[...] = matmul(rows_ref[...], cols_ref[theirs, :], ((1,), (1,))).astype(BF16)
@@ -185,7 +186,7 @@
     half = sketch_rows // 2
     size = width // (n * n)
 
-    own = send_all(spread(whitener, n), RING).reshape(half, sketch_rows)
+    own = send_all(spread(whitener, n), ("y_hi", "x")).reshape(half, sketch_rows)
 
     keep, give = project(core, grads, projection)
     got = lax.ppermute(give, "core", SWAP)
@@ -202,8 +203,13 @@
     shape = jax.ShapeDtypeStruct((n * size, half), F32)
     first = call(first_half_kernel, shape, flops, core, mine, own, name="first_half")
     shape = jax.ShapeDtypeStruct((n * n, 2 * size, half), BF16)
-    copies = call(whiten_kernel, shape, flops, core, first, theirs, own, name="whiten")
-    pieces = send_all(copies, chips)
+    depth = lax.axis_size("z")
+    places = [[(e // depth * n + q) * depth + e % depth for e in range(n)] for q in range(n)]
+    copies = call(
+        lambda *refs: whiten_kernel(*refs, places=places),
+        shape, flops, core, first, theirs, own, name="whiten",
+    )
+    pieces = send_all(copies, ("y_lo", "x", "y_hi", "z"))
     across = width // lax.axis_size("core")
     flops = 2 * width * across * half
     shapes = (
@@ -211,7 +217,10 @@
         jax.ShapeDtypeStruct((width, half), BF16),
         jax.ShapeDtypeStruct((width, half), BF16),
     )
-    give, rows, cols = call(give_kernel, shapes, flops, core, pieces, name="give")
+    give, rows, cols = call(
+        lambda *refs: give_kernel(*refs, places=places),
+        shapes, flops, core, pieces, name="give",
+    )
     got = lax.ppermute(give, "core", SWAP)
     shape = jax.ShapeDtypeStruct((width, across), F32)
     keep = call(keep_kernel, shape, flops, core, rows, cols, name="keep")

time: 75.9 us -> 75.6 us (level)
  blocking collectives: 41.4 us -> 39.4 us
  waiting for transfers between devices: 5.68 us -> 7.5 us
    all_to_all x2, blocking collectives: 41.4 us -> 39.4 us  [send_all(): return lax.all_to_all(copies, axes, 0, 0, tiled=True)]
    all_to_all x1, waiting for transfers between devices: 2.64 us -> 4.47 us  [send_all(): return lax.all_to_all(copies, axes, 0, 0, tiled=True)]
  transfers between devices with their start and end apart: 4 -> 4, of which waited for: 4 -> 4; matrix products, arithmetic and copies ran while one was open for 0% -> 0% of each run, Pallas kernels for 14% -> 15%
where the time goes in v4:
time: 75.6 us; the launch traced here: 75.3 us
  blocking collectives  39.4 us (52%)
  Pallas kernels  13.8 us (18%)
  starting transfers between devices  13.6 us (18%)
  waiting for transfers between devices  7.5 us (10%)
  other arithmetic  1.01 us (1%)
    all_to_all x2, blocking collectives, send_all(): return lax.all_to_all(copies, axes, 0, 0, tiled=True)  39.4 us
    pallas_call x1, Pallas kernels, project(): pl.pallas_call(project_kernel, out_shape=(jax.ShapeDtypeStruct((width, ha...  10.3 us
    all_to_all x1, starting transfers between devices, send_all(): return lax.all_to_all(copies, axes, 0, 0, tiled=True)  7.48 us
    all_to_all x1, waiting for transfers between devices, send_all(): return lax.all_to_all(copies, axes, 0, 0, tiled=True)  4.47 us
    ppermute x2, starting transfers between devices, body(): got = lax.ppermute(give, 'core', SWAP)  3.58 us
    ppermute x1, starting transfers between devices, body(): theirs = lax.ppermute(mine, 'core', SWAP)  2.55 us
    ppermute x2, waiting for transfers between devices, body(): got = lax.ppermute(give, 'core', SWAP)  2.36 us
    pallas_call x1, Pallas kernels, spread(): pl.pallas_call(spread_kernel, out_shape=jax.ShapeDtypeStruct((count,) + p...  1.99 us
  transfers between devices with their start and end apart: 4, of which 4 were waited for; matrix products, arithmetic and copies ran while one was open for 0% of the time, Pallas kernels for 15%

profile of v4, /device:TPU:1, one launch (start us, length us, event | category | flops | bytes accessed | tf_op | source)
XLA Modules:
  0.0 75.3 jit_solution(13068817477476563458)
XLA Ops:
  0.0 2.0 %spread.1 = bf16[8,64,1024]{2,1,0:T(8,128)(2,1)} custom-call(f32[64,1024]{1,0:T(8,128)} %part_ref.1), custom_call_target="tpu_custom_call" | custom-call | tf_op jit(solution)/shard_map/spread/pallas_call | solution.py:102
  2.0 7.5 %all-to-all-start = ((bf16[8,64,1024]{2,1,0:T(8,128)(2,1)}), bf16[8,64,1024]{2,1,0:T(8,128)(2,1)S(1)}, u32[]{:S(2)}, u32[]{:S(2)}) async-start(bf16[8,64,1024]{2,1,0:T(8,128)(2,1)} %spread.1), calls=%async_computation | async-start | bytes 2097152 | tf_op jit(solution)/shard_map/all_to_all | solution.py:24
  9.5 10.3 %project.1 = (f32[512,512]{1,0:T(8,128)S(1)}, bf16[512,512]{1,0:T(8,128)(2,1)S(1)}) custom-call(s32[1]{0:T(128)} %bitcast.core_ref.refs_0_, f32[6144,512]{1,0:T(8,128)} %grads_hbm.1, bf16[6144,1024]{1,0:T(8,128)(2,1)} %projection_hbm.1), custom_call_target="tpu_custom_call" | custom-call | flops 6442450944 | bytes 25165824 | tf_op jit(solution)/shard_map/project/pallas_call | solution.py:71
  19.8 1.0 %collective-permute-start = (bf16[512,512]{1,0:T(8,128)(2,1)S(1)}, bf16[512,512]{1,0:T(8,128)(2,1)S(1)}, u32[]{:S(2)}, u32[]{:S(2)}) collective-permute-start(bf16[512,512]{1,0:T(8,128)(2,1)S(1)} %get-tuple-element.13), channel_id=1, source_target_pairs={{0,8},{8,0},{1,9},{9,1},{2,10},{10,2},{3,11},{11,3},{4,12},{12,4},... | collective-permute-start | bytes 1572872 | tf_op jit(solution)/shard_map/ppermute | solution.py:192
  20.8 1.5 %collective-permute-done = bf16[512,512]{1,0:T(8,128)(2,1)S(1)} collective-permute-done((bf16[512,512]{1,0:T(8,128)(2,1)S(1)}, bf16[512,512]{1,0:T(8,128)(2,1)S(1)}, u32[]{:S(2)}, u32[]{:S(2)}) %collective-permute-start) | collective-permute-done | bytes 524320 | tf_op jit(solution)/shard_map/ppermute | solution.py:192
  22.3 4.5 %all-to-all-done = bf16[8,64,1024]{2,1,0:T(8,128)(2,1)S(1)} async-done(((bf16[8,64,1024]{2,1,0:T(8,128)(2,1)}), bf16[8,64,1024]{2,1,0:T(8,128)(2,1)S(1)}, u32[]{:S(2)}, u32[]{:S(2)}) %all-to-all-start) | async-done | bytes 1048608 | tf_op jit(solution)/shard_map/all_to_all | solution.py:24
  26.8 0.2 fusion
  26.9 18.3 %all_to_all.15.refs_1_ = bf16[64,8,512]{2,1,0:T(8,128)(2,1)S(1)} all-to-all(bf16[64,8,512]{2,1,0:T(8,128)(2,1)S(1)} %fusion), channel_id=1, replica_groups=mesh['x'=4,'y_hi'=2,'core'=2,'y_lo'=2,'z'=4] {'x','y_hi','y_lo','z'}, dimensions={0} | all-to-all | bytes 1048576 | tf_op jit(solution)/shard_map/all_to_all | solution.py:24
  45.3 0.1 reduce.1.mine_ref
  45.4 2.6 %collective-permute-start.1 = (f32[64,512]{1,0:T(8,128)S(1)}, f32[64,512]{1,0:T(8,128)S(1)}, u32[]{:S(2)}, u32[]{:S(2)}) collective-permute-start(f32[64,512]{1,0:T(8,128)S(1)} %reduce.1.mine_ref), channel_id=1, source_target_pairs={{0,8},{8,0},{1,9},{9,1},{2,10},{10,2},{3,11},{11,3},{4,12},{12,4},... | collective-permute-start | bytes 393224 | tf_op jit(solution)/shard_map/ppermute | solution.py:201
  47.9 0.3 first_half.1.refs_1_
  48.2 0.7 collective-permute-done.1.refs_2_
  48.9 0.4 whiten.1
  49.3 21.1 %all_to_all.16.refs_1_ = bf16[64,16,512]{2,1,0:T(8,128)(2,1)S(1)} all-to-all(bf16[64,16,512]{2,1,0:T(8,128)(2,1)S(1)} %whiten.1), channel_id=1, replica_groups=mesh['x'=4,'y_hi'=2,'core'=2,'y_lo'=2,'z'=4] {'y_lo','x','y_hi','z'}, dimensions={0} | all-to-all | bytes 2097152 | tf_op jit(solution)/shard_map/all_to_all | solution.py:24
  70.4 0.4 give.1
  70.7 2.6 %collective-permute-start.2 = (bf16[512,256]{1,0:T(8,128)(2,1)S(1)}, bf16[512,256]{1,0:T(8,128)(2,1)S(1)}, u32[]{:S(2)}, u32[]{:S(2)}) collective-permute-start(bf16[512,256]{1,0:T(8,128)(2,1)S(1)} %get-tuple-element.18), channel_id=1, source_target_pairs={{0,8},{8,0},{1,9},{9,1},{2,10},{10,2},{3,11},{11,3},{4,12},{12,4},... | collective-permute-start | bytes 786440 | tf_op jit(solution)/shard_map/ppermute | solution.py:224
  73.3 0.3 keep.1
  73.7 0.8 %collective-permute-done.2 = bf16[512,256]{1,0:T(8,128)(2,1)S(1)} collective-permute-done((bf16[512,256]{1,0:T(8,128)(2,1)S(1)}, bf16[512,256]{1,0:T(8,128)(2,1)S(1)}, u32[]{:S(2)}, u32[]{:S(2)}) %collective-permute-start.2) | collective-permute-done | bytes 262176 | tf_op jit(solution)/shard_map/ppermute | solution.py:224
  74.5 0.8 %add_multiply_fusion = f32[512,256]{1,0:T(8,128)} fusion(f32[512,256]{1,0:T(8,128)S(1)} %keep.1, bf16[512,256]{1,0:T(8,128)(2,1)S(1)} %collective-permute-done.2), kind=kLoop, calls=%fused_computation.2 | loop fusion | flops 393216 | bytes 1310720 | tf_op jit(solution)/shard_map/mul | solution.py:227
Async XLA Ops:
  2.0 24.8 %all-to-all-start = ((bf16[8,64,1024]{2,1,0:T(8,128)(2,1)}), bf16[8,64,1024]{2,1,0:T(8,128)(2,1)S(1)}, u32[]{:S(2)}, u32[]{:S(2)}) async-start(bf16[8,64,1024]{2,1,0:T(8,128)(2,1)} %spread.1), calls=%async_computation | async-start | bytes 2097152 | tf_op jit(solution)/shard_map/all_to_all | solution.py:24
  19.8 2.5 %collective-permute-start = (bf16[512,512]{1,0:T(8,128)(2,1)S(1)}, bf16[512,512]{1,0:T(8,128)(2,1)S(1)}, u32[]{:S(2)}, u32[]{:S(2)}) collective-permute-start(bf16[512,512]{1,0:T(8,128)(2,1)S(1)} %get-tuple-element.13), channel_id=1, source_target_pairs={{0,8},{8,0},{1,9},{9,1},{2,10},{10,2},{3,11},{11,3},{4,12},{12,4},... | collective-permute-start | bytes 1572872 | tf_op jit(solution)/shard_map/ppermute | solution.py:192
  45.4 3.5 %collective-permute-start.1 = (f32[64,512]{1,0:T(8,128)S(1)}, f32[64,512]{1,0:T(8,128)S(1)}, u32[]{:S(2)}, u32[]{:S(2)}) collective-permute-start(f32[64,512]{1,0:T(8,128)S(1)} %reduce.1.mine_ref), channel_id=1, source_target_pairs={{0,8},{8,0},{1,9},{9,1},{2,10},{10,2},{3,11},{11,3},{4,12},{12,4},... | collective-permute-start | bytes 393224 | tf_op jit(solution)/shard_map/ppermute | solution.py:201
  70.7 3.8 %collective-permute-start.2 = (bf16[512,256]{1,0:T(8,128)(2,1)S(1)}, bf16[512,256]{1,0:T(8,128)(2,1)S(1)}, u32[]{:S(2)}, u32[]{:S(2)}) collective-permute-start(bf16[512,256]{1,0:T(8,128)(2,1)S(1)} %get-tuple-element.18), channel_id=1, source_target_pairs={{0,8},{8,0},{1,9},{9,1},{2,10},{10,2},{3,11},{11,3},{4,12},{12,4},... | collective-permute-start | bytes 786440 | tf_op jit(solution)/shard_map/ppermute | solution.py:224

commit v5 on v4

--- a/solution.py
+++ b/solution.py
@@ -14,6 +14,7 @@
 SWAP = [(0, 1), (1, 0)]
 TILE = 512
 STEPS = (1, 2, 3, 3, 2, 1)
+TAIL = 3
 
 
 def matmul(a, b, dims):
@@ -25,19 +26,28 @@
 
 
 def project_kernel(
-    core_ref, grads_hbm, projection_hbm, keep_ref, give_ref, grads_ref, projection_ref, total, sems
+    core_ref, grads_hbm, projection_hbm, keep_ref, give_ref, grads_tail, projection_tail,
+    grads_ref, projection_ref, total, sems,
 ):
     rows = grads_ref.shape[0]
     half = keep_ref.shape[1]
+    head = rows - grads_tail.shape[0]
     mine = pl.ds(pl.multiple_of(core_ref[0] * half, half), half)
     theirs = pl.ds(pl.multiple_of((1 - core_ref[0]) * half, half), half)
     copies = []
     for i in range(rows // TILE):
         part = pl.ds(i * TILE, TILE)
-        pair = (
-            pltpu.make_async_copy(grads_hbm.at[part], grads_ref.at[part], sems.at[0, i]),
-            pltpu.make_async_copy(projection_hbm.at[part], projection_ref.at[part], sems.at[1, i]),
-        )
+        pair = [pltpu.make_async_copy(grads_hbm.at[part], grads_ref.at[part], sems.at[0, i])]
+        if i * TILE < head:
+            target = projection_ref.at[part]
+            pair.append(pltpu.make_async_copy(projection_hbm.at[part], target, sems.at[1, i]))
+        else:
+            target = projection_ref.at[part, pl.ds(0, half)]
+            source = projection_hbm.at[part, theirs]
+            pair.append(pltpu.make_async_copy(source, target, sems.at[1, i]))
+            target = projection_tail.at[pl.ds(i * TILE - head, TILE)]
+            source = projection_hbm.at[part, mine]
+            pair.append(pltpu.make_async_copy(source, target, sems.at[2, i]))
         for copy in pair:
             copy.start()
         copies.append(pair)
@@ -46,20 +56,26 @@
         for pair in copies[first : first + count]:
             for copy in pair:
                 copy.wait()
-        part = pl.ds(first * TILE, count * TILE)
+        start = first * TILE
+        part = pl.ds(start, count * TILE)
         grads = grads_ref[part, :].astype(BF16)
-        near = matmul(grads, projection_ref[part, mine], ((0,), (0,)))
-        far = matmul(grads, projection_ref[part, theirs], ((0,), (0,)))
         first += count
-        if first == count:
-            keep_ref[...] = near
-            total[...] = far
-        elif first < rows // TILE:
-            keep_ref[...] += near
-            total[...] += far
+        if start < head:
+            near = matmul(grads, projection_ref[part, mine], ((0,), (0,)))
+            far = matmul(grads, projection_ref[part, theirs], ((0,), (0,)))
+            if start == 0:
+                keep_ref[...] = near
+                total[...] = far
+            else:
+                keep_ref[...] += near
+                total[...] += far
         else:
-            keep_ref[...] += near
-            give_ref[...] = (total[...] + far).astype(BF16)
+            grads_tail[pl.ds(start - head, count * TILE), :] = grads
+            far = matmul(grads, projection_ref[part, :half], ((0,), (0,)))
+            if first < rows // TILE:
+                total[...] += far
+            else:
+                give_ref[...] = (total[...] + far).astype(BF16)
 
 
 def project(core, grads, projection):
@@ -73,16 +89,18 @@
         out_shape=(
             jax.ShapeDtypeStruct((width, half), F32),
             jax.ShapeDtypeStruct((width, half), BF16),
+            jax.ShapeDtypeStruct((TAIL * TILE, width), BF16),
+            jax.ShapeDtypeStruct((TAIL * TILE, half), projection.dtype),
         ),
         in_specs=[pl.BlockSpec(memory_space=pltpu.SMEM), hbm, hbm],
-        out_specs=[vmem, vmem],
+        out_specs=[vmem] * 4,
         scratch_shapes=[
             pltpu.VMEM((rows, width), grads.dtype),
             pltpu.VMEM((rows, cols), projection.dtype),
             pltpu.VMEM((width, half), F32),
-            pltpu.SemaphoreType.DMA((2, rows // TILE)),
+            pltpu.SemaphoreType.DMA((3, rows // TILE)),
         ],
-        compiler_params=pltpu.CompilerParams(vmem_limit_bytes=52 << 20),
+        compiler_params=pltpu.CompilerParams(vmem_limit_bytes=48 << 20),
         cost_estimate=pl.CostEstimate(
             flops=2 * rows * width * cols,
             bytes_accessed=rows * (4 * width + 2 * cols),
@@ -90,6 +108,10 @@
         ),
         name="project",
     )(core, grads, projection)
+
+
+def tail_kernel(core_ref, keep_ref, grads_ref, projection_ref, out_ref):
+    out_ref[...] = keep_ref[...] + matmul(grads_ref[...], projection_ref[...], ((0,), (0,)))
 
 
 def spread_kernel(part_ref, out_ref):
@@ -188,8 +210,11 @@
 
     own = send_all(spread(whitener, n), ("y_hi", "x")).reshape(half, sketch_rows)
 
-    keep, give = project(core, grads, projection)
+    keep, give, *tail = project(core, grads, projection)
     got = lax.ppermute(give, "core", SWAP)
+    shape = jax.ShapeDtypeStruct(keep.shape, F32)
+    flops = 2 * TAIL * TILE * width * half
+    keep = call(tail_kernel, shape, flops, core, keep, *tail, name="tail")
     got, own = lax.optimization_barrier((got, own))
     blocks = (keep + got.astype(F32)).astype(BF16)
     pieces = send_all(blocks.reshape(n * n, size, half), chips)

time: 75.6 us -> 75.5 us (level)
    pallas_call x5 -> x6, Pallas kernels: 1.44 us -> 2.44 us  [call(): pl.pallas_call(kernel, out_shape=out_shape, in_specs=[pl.BlockSpec(memory...]
    ppermute x2, waiting for transfers between devices: 2.36 us -> 1.37 us  [body(): got = lax.ppermute(give, 'core', SWAP)]
where the time goes in v5:
time: 75.5 us; the launch traced here: 75.2 us
  blocking collectives  39.1 us (52%)
  Pallas kernels  14 us (19%)
  starting transfers between devices  13.8 us (18%)
  waiting for transfers between devices  7.21 us (10%)
  other arithmetic  1.01 us (1%)
    all_to_all x2, blocking collectives, send_all(): return lax.all_to_all(copies, axes, 0, 0, tiled=True)  39.1 us
    pallas_call x1, Pallas kernels, project(): pl.pallas_call(project_kernel, out_shape=(jax.ShapeDtypeStruct((width, ha...  9.58 us
    all_to_all x1, starting transfers between devices, send_all(): return lax.all_to_all(copies, axes, 0, 0, tiled=True)  7.48 us
    all_to_all x1, waiting for transfers between devices, send_all(): return lax.all_to_all(copies, axes, 0, 0, tiled=True)  5.17 us
    ppermute x2, starting transfers between devices, body(): got = lax.ppermute(give, 'core', SWAP)  3.61 us
    ppermute x1, starting transfers between devices, body(): theirs = lax.ppermute(mine, 'core', SWAP)  2.7 us
    pallas_call x6, Pallas kernels, call(): pl.pallas_call(kernel, out_shape=out_shape, in_specs=[pl.BlockSpec(memory...  2.44 us
    pallas_call x1, Pallas kernels, spread(): pl.pallas_call(spread_kernel, out_shape=jax.ShapeDtypeStruct((count,) + p...  1.99 us
  transfers between devices with their start and end apart: 4, of which 4 were waited for; matrix products, arithmetic and copies ran while one was open for 0% of the time, Pallas kernels for 15%

profile of v5, /device:TPU:1, one launch (start us, length us, event | category | flops | bytes accessed | tf_op | source)
XLA Modules:
  0.0 75.2 jit_solution(10376013291395780425)
XLA Ops:
  0.0 2.0 %spread.1 = bf16[8,64,1024]{2,1,0:T(8,128)(2,1)} custom-call(f32[64,1024]{1,0:T(8,128)} %part_ref.1), custom_call_target="tpu_custom_call" | custom-call | tf_op jit(solution)/shard_map/spread/pallas_call | solution.py:124
  2.0 7.5 %all-to-all-start = ((bf16[8,64,1024]{2,1,0:T(8,128)(2,1)}), bf16[8,64,1024]{2,1,0:T(8,128)(2,1)S(1)}, u32[]{:S(2)}, u32[]{:S(2)}) async-start(bf16[8,64,1024]{2,1,0:T(8,128)(2,1)} %spread.1), calls=%async_computation | async-start | bytes 2097152 | tf_op jit(solution)/shard_map/all_to_all | solution.py:25
  9.5 9.6 %project.1 = (f32[512,512]{1,0:T(8,128)S(1)}, bf16[512,512]{1,0:T(8,128)(2,1)S(1)}, bf16[1536,512]{1,0:T(8,128)(2,1)S(1)}, bf16[1536,512]{1,0:T(8,128)(2,1)S(1)}) custom-call(s32[1]{0:T(128)} %bitcast.core_ref.refs_0_, f32[6144,512]{1,0:T(8,128)} %grads_hbm.1, bf16[6144,1024]{1,0:T(8,128)(2,1)} %projection_hbm.1), custom_call_target="tpu_custom_call" | custom-call | flops 6442450944 | bytes 25165824 | tf_op jit(solution)/shard_map/project/pallas_call | solution.py:87
  19.1 1.0 %collective-permute-start = (bf16[512,512]{1,0:T(8,128)(2,1)S(1)}, bf16[512,512]{1,0:T(8,128)(2,1)S(1)}, u32[]{:S(2)}, u32[]{:S(2)}) collective-permute-start(bf16[512,512]{1,0:T(8,128)(2,1)S(1)} %get-tuple-element.17), channel_id=1, source_target_pairs={{0,8},{8,0},{1,9},{9,1},{2,10},{10,2},{3,11},{11,3},{4,12},{12,4},... | collective-permute-start | bytes 1572872 | tf_op jit(solution)/shard_map/ppermute | solution.py:214
  20.1 1.0 %tail.1 = f32[512,512]{1,0:T(8,128)S(1)} custom-call(s32[1]{0:T(128)} %bitcast.core_ref.refs_0_, f32[512,512]{1,0:T(8,128)S(1)} %get-tuple-element.14.keep_ref, bf16[1536,512]{1,0:T(8,128)(2,1)S(1)} %get-tuple-element.15.grads_ref, bf16[1536,512]{1,0:T(8,128)(2,1)S(1)} %get-tuple-element.16.projection_ref), custom_call_target="tpu_custom_call" | custom-call | flops 805306368 | bytes 4194304 | tf_op jit(solution)/shard_map/tail/pallas_call | solution.py:136
  21.1 0.5 collective-permute-done
  21.6 5.2 %all-to-all-done = bf16[8,64,1024]{2,1,0:T(8,128)(2,1)S(1)} async-done(((bf16[8,64,1024]{2,1,0:T(8,128)(2,1)}), bf16[8,64,1024]{2,1,0:T(8,128)(2,1)S(1)}, u32[]{:S(2)}, u32[]{:S(2)}) %all-to-all-start) | async-done | bytes 1048608 | tf_op jit(solution)/shard_map/all_to_all | solution.py:25
  26.8 0.2 fusion
  26.9 18.0 %all_to_all.15.refs_1_ = bf16[64,8,512]{2,1,0:T(8,128)(2,1)S(1)} all-to-all(bf16[64,8,512]{2,1,0:T(8,128)(2,1)S(1)} %fusion), channel_id=1, replica_groups=mesh['x'=4,'y_hi'=2,'core'=2,'y_lo'=2,'z'=4] {'x','y_hi','y_lo','z'}, dimensions={0} | all-to-all | bytes 1048576 | tf_op jit(solution)/shard_map/all_to_all | solution.py:25
  45.0 0.1 reduce.1.mine_ref
  45.1 2.7 %collective-permute-start.1 = (f32[64,512]{1,0:T(8,128)S(1)}, f32[64,512]{1,0:T(8,128)S(1)}, u32[]{:S(2)}, u32[]{:S(2)}) collective-permute-start(f32[64,512]{1,0:T(8,128)S(1)} %reduce.1.mine_ref), channel_id=1, source_target_pairs={{0,8},{8,0},{1,9},{9,1},{2,10},{10,2},{3,11},{11,3},{4,12},{12,4},... | collective-permute-start | bytes 393224 | tf_op jit(solution)/shard_map/ppermute | solution.py:226
  47.8 0.3 first_half.1.refs_1_
  48.1 0.7 collective-permute-done.1.refs_2_
  48.7 0.4 whiten.1
  49.1 21.1 %all_to_all.16.refs_1_ = bf16[64,16,512]{2,1,0:T(8,128)(2,1)S(1)} all-to-all(bf16[64,16,512]{2,1,0:T(8,128)(2,1)S(1)} %whiten.1), channel_id=1, replica_groups=mesh['x'=4,'y_hi'=2,'core'=2,'y_lo'=2,'z'=4] {'y_lo','x','y_hi','z'}, dimensions={0} | all-to-all | bytes 2097152 | tf_op jit(solution)/shard_map/all_to_all | solution.py:25
  70.2 0.4 give.1
  70.6 2.6 %collective-permute-start.2 = (bf16[512,256]{1,0:T(8,128)(2,1)S(1)}, bf16[512,256]{1,0:T(8,128)(2,1)S(1)}, u32[]{:S(2)}, u32[]{:S(2)}) collective-permute-start(bf16[512,256]{1,0:T(8,128)(2,1)S(1)} %get-tuple-element.22), channel_id=1, source_target_pairs={{0,8},{8,0},{1,9},{9,1},{2,10},{10,2},{3,11},{11,3},{4,12},{12,4},... | collective-permute-start | bytes 786440 | tf_op jit(solution)/shard_map/ppermute | solution.py:249
  73.2 0.3 keep.1
  73.5 0.8 %collective-permute-done.2 = bf16[512,256]{1,0:T(8,128)(2,1)S(1)} collective-permute-done((bf16[512,256]{1,0:T(8,128)(2,1)S(1)}, bf16[512,256]{1,0:T(8,128)(2,1)S(1)}, u32[]{:S(2)}, u32[]{:S(2)}) %collective-permute-start.2) | collective-permute-done | bytes 262176 | tf_op jit(solution)/shard_map/ppermute | solution.py:249
  74.4 0.8 %add_multiply_fusion = f32[512,256]{1,0:T(8,128)} fusion(f32[512,256]{1,0:T(8,128)S(1)} %keep.1, bf16[512,256]{1,0:T(8,128)(2,1)S(1)} %collective-permute-done.2), kind=kLoop, calls=%fused_computation.2 | loop fusion | flops 393216 | bytes 1310720 | tf_op jit(solution)/shard_map/mul | solution.py:252
Async XLA Ops:
  2.0 24.8 %all-to-all-start = ((bf16[8,64,1024]{2,1,0:T(8,128)(2,1)}), bf16[8,64,1024]{2,1,0:T(8,128)(2,1)S(1)}, u32[]{:S(2)}, u32[]{:S(2)}) async-start(bf16[8,64,1024]{2,1,0:T(8,128)(2,1)} %spread.1), calls=%async_computation | async-start | bytes 2097152 | tf_op jit(solution)/shard_map/all_to_all | solution.py:25
  19.1 2.6 %collective-permute-start = (bf16[512,512]{1,0:T(8,128)(2,1)S(1)}, bf16[512,512]{1,0:T(8,128)(2,1)S(1)}, u32[]{:S(2)}, u32[]{:S(2)}) collective-permute-start(bf16[512,512]{1,0:T(8,128)(2,1)S(1)} %get-tuple-element.17), channel_id=1, source_target_pairs={{0,8},{8,0},{1,9},{9,1},{2,10},{10,2},{3,11},{11,3},{4,12},{12,4},... | collective-permute-start | bytes 1572872 | tf_op jit(solution)/shard_map/ppermute | solution.py:214
  45.1 3.7 %collective-permute-start.1 = (f32[64,512]{1,0:T(8,128)S(1)}, f32[64,512]{1,0:T(8,128)S(1)}, u32[]{:S(2)}, u32[]{:S(2)}) collective-permute-start(f32[64,512]{1,0:T(8,128)S(1)} %reduce.1.mine_ref), channel_id=1, source_target_pairs={{0,8},{8,0},{1,9},{9,1},{2,10},{10,2},{3,11},{11,3},{4,12},{12,4},... | collective-permute-start | bytes 393224 | tf_op jit(solution)/shard_map/ppermute | solution.py:226
  70.6 3.8 %collective-permute-start.2 = (bf16[512,256]{1,0:T(8,128)(2,1)S(1)}, bf16[512,256]{1,0:T(8,128)(2,1)S(1)}, u32[]{:S(2)}, u32[]{:S(2)}) collective-permute-start(bf16[512,256]{1,0:T(8,128)(2,1)S(1)} %get-tuple-element.22), channel_id=1, source_target_pairs={{0,8},{8,0},{1,9},{9,1},{2,10},{10,2},{3,11},{11,3},{4,12},{12,4},... | collective-permute-start | bytes 786440 | tf_op jit(solution)/shard_map/ppermute | solution.py:249

commit v6 on v5

--- a/solution.py
+++ b/solution.py
@@ -208,7 +208,7 @@
     half = sketch_rows // 2
     size = width // (n * n)
 
-    own = send_all(spread(whitener, n), ("y_hi", "x")).reshape(half, sketch_rows)
+    own = send_all(spread(whitener, n), RING).reshape(half, sketch_rows)
 
     keep, give, *tail = project(core, grads, projection)
     got = lax.ppermute(give, "core", SWAP)

time: 75.5 us -> 75.4 us (level)
  waiting for transfers between devices: 7.21 us -> 5.37 us
  blocking collectives: 39.1 us -> 40.9 us
    all_to_all x1, waiting for transfers between devices: 5.17 us -> 3.34 us  [send_all(): return lax.all_to_all(copies, axes, 0, 0, tiled=True)]
    all_to_all x2, blocking collectives: 39.1 us -> 40.9 us  [send_all(): return lax.all_to_all(copies, axes, 0, 0, tiled=True)]
where the time goes in v6:
time: 75.4 us; the launch traced here: 75.2 us
  blocking collectives  40.9 us (54%)
  Pallas kernels  14 us (19%)
  starting transfers between devices  13.8 us (18%)
  waiting for transfers between devices  5.37 us (7%)
  other arithmetic  1.01 us (1%)
    all_to_all x2, blocking collectives, send_all(): return lax.all_to_all(copies, axes, 0, 0, tiled=True)  40.9 us
    pallas_call x1, Pallas kernels, project(): pl.pallas_call(project_kernel, out_shape=(jax.ShapeDtypeStruct((width, ha...  9.58 us
    all_to_all x1, starting transfers between devices, send_all(): return lax.all_to_all(copies, axes, 0, 0, tiled=True)  7.48 us
    ppermute x2, starting transfers between devices, body(): got = lax.ppermute(give, 'core', SWAP)  3.6 us
    all_to_all x1, waiting for transfers between devices, send_all(): return lax.all_to_all(copies, axes, 0, 0, tiled=True)  3.34 us
    ppermute x1, starting transfers between devices, body(): theirs = lax.ppermute(mine, 'core', SWAP)  2.71 us
    pallas_call x6, Pallas kernels, call(): pl.pallas_call(kernel, out_shape=out_shape, in_specs=[pl.BlockSpec(memory...  2.47 us
    pallas_call x1, Pallas kernels, spread(): pl.pallas_call(spread_kernel, out_shape=jax.ShapeDtypeStruct((count,) + p...  1.99 us
  transfers between devices with their start and end apart: 4, of which 4 were waited for; matrix products, arithmetic and copies ran while one was open for 0% of the time, Pallas kernels for 15%

profile of v6, /device:TPU:1, one launch (start us, length us, event | category | flops | bytes accessed | tf_op | source)
XLA Modules:
  0.0 75.2 jit_solution(729799627753461571)
XLA Ops:
  0.0 2.0 %spread.1 = bf16[8,64,1024]{2,1,0:T(8,128)(2,1)} custom-call(f32[64,1024]{1,0:T(8,128)} %part_ref.1), custom_call_target="tpu_custom_call" | custom-call | tf_op jit(solution)/shard_map/spread/pallas_call | solution.py:124
  2.0 7.5 %all-to-all-start = ((bf16[8,64,1024]{2,1,0:T(8,128)(2,1)}), bf16[8,64,1024]{2,1,0:T(8,128)(2,1)S(1)}, u32[]{:S(2)}, u32[]{:S(2)}) async-start(bf16[8,64,1024]{2,1,0:T(8,128)(2,1)} %spread.1), calls=%async_computation | async-start | bytes 2097152 | tf_op jit(solution)/shard_map/all_to_all | solution.py:25
  9.5 9.6 %project.1 = (f32[512,512]{1,0:T(8,128)S(1)}, bf16[512,512]{1,0:T(8,128)(2,1)S(1)}, bf16[1536,512]{1,0:T(8,128)(2,1)S(1)}, bf16[1536,512]{1,0:T(8,128)(2,1)S(1)}) custom-call(s32[1]{0:T(128)} %bitcast.core_ref.refs_0_, f32[6144,512]{1,0:T(8,128)} %grads_hbm.1, bf16[6144,1024]{1,0:T(8,128)(2,1)} %projection_hbm.1), custom_call_target="tpu_custom_call" | custom-call | flops 6442450944 | bytes 25165824 | tf_op jit(solution)/shard_map/project/pallas_call | solution.py:87
  19.1 1.0 %collective-permute-start = (bf16[512,512]{1,0:T(8,128)(2,1)S(1)}, bf16[512,512]{1,0:T(8,128)(2,1)S(1)}, u32[]{:S(2)}, u32[]{:S(2)}) collective-permute-start(bf16[512,512]{1,0:T(8,128)(2,1)S(1)} %get-tuple-element.17), channel_id=1, source_target_pairs={{0,8},{8,0},{1,9},{9,1},{2,10},{10,2},{3,11},{11,3},{4,12},{12,4},... | collective-permute-start | bytes 1572872 | tf_op jit(solution)/shard_map/ppermute | solution.py:214
  20.1 1.0 %tail.1 = f32[512,512]{1,0:T(8,128)S(1)} custom-call(s32[1]{0:T(128)} %bitcast.core_ref.refs_0_, f32[512,512]{1,0:T(8,128)S(1)} %get-tuple-element.14.keep_ref, bf16[1536,512]{1,0:T(8,128)(2,1)S(1)} %get-tuple-element.15.grads_ref, bf16[1536,512]{1,0:T(8,128)(2,1)S(1)} %get-tuple-element.16.projection_ref), custom_call_target="tpu_custom_call" | custom-call | flops 805306368 | bytes 4194304 | tf_op jit(solution)/shard_map/tail/pallas_call | solution.py:136
  21.1 0.5 collective-permute-done
  21.6 3.3 %all-to-all-done = bf16[8,64,1024]{2,1,0:T(8,128)(2,1)S(1)} async-done(((bf16[8,64,1024]{2,1,0:T(8,128)(2,1)}), bf16[8,64,1024]{2,1,0:T(8,128)(2,1)S(1)}, u32[]{:S(2)}, u32[]{:S(2)}) %all-to-all-start) | async-done | bytes 1048608 | tf_op jit(solution)/shard_map/all_to_all | solution.py:25
  25.0 0.2 fusion
  25.1 19.8 %all_to_all.15.refs_1_ = bf16[64,8,512]{2,1,0:T(8,128)(2,1)S(1)} all-to-all(bf16[64,8,512]{2,1,0:T(8,128)(2,1)S(1)} %fusion), channel_id=1, replica_groups=mesh['x'=4,'y_hi'=2,'core'=2,'y_lo'=2,'z'=4] {'x','y_hi','y_lo','z'}, dimensions={0} | all-to-all | bytes 1048576 | tf_op jit(solution)/shard_map/all_to_all | solution.py:25
  44.9 0.1 reduce.1.mine_ref
  45.0 2.7 %collective-permute-start.1 = (f32[64,512]{1,0:T(8,128)S(1)}, f32[64,512]{1,0:T(8,128)S(1)}, u32[]{:S(2)}, u32[]{:S(2)}) collective-permute-start(f32[64,512]{1,0:T(8,128)S(1)} %reduce.1.mine_ref), channel_id=1, source_target_pairs={{0,8},{8,0},{1,9},{9,1},{2,10},{10,2},{3,11},{11,3},{4,12},{12,4},... | collective-permute-start | bytes 393224 | tf_op jit(solution)/shard_map/ppermute | solution.py:226
  47.7 0.3 first_half.1.refs_1_
  48.0 0.7 collective-permute-done.1.refs_2_
  48.7 0.4 whiten.1
  49.1 21.1 %all_to_all.16.refs_1_ = bf16[64,16,512]{2,1,0:T(8,128)(2,1)S(1)} all-to-all(bf16[64,16,512]{2,1,0:T(8,128)(2,1)S(1)} %whiten.1), channel_id=1, replica_groups=mesh['x'=4,'y_hi'=2,'core'=2,'y_lo'=2,'z'=4] {'y_lo','x','y_hi','z'}, dimensions={0} | all-to-all | bytes 2097152 | tf_op jit(solution)/shard_map/all_to_all | solution.py:25
  70.2 0.4 give.1
  70.6 2.6 %collective-permute-start.2 = (bf16[512,256]{1,0:T(8,128)(2,1)S(1)}, bf16[512,256]{1,0:T(8,128)(2,1)S(1)}, u32[]{:S(2)}, u32[]{:S(2)}) collective-permute-start(bf16[512,256]{1,0:T(8,128)(2,1)S(1)} %get-tuple-element.22), channel_id=1, source_target_pairs={{0,8},{8,0},{1,9},{9,1},{2,10},{10,2},{3,11},{11,3},{4,12},{12,4},... | collective-permute-start | bytes 786440 | tf_op jit(solution)/shard_map/ppermute | solution.py:249
  73.2 0.3 keep.1
  73.5 0.8 %collective-permute-done.2 = bf16[512,256]{1,0:T(8,128)(2,1)S(1)} collective-permute-done((bf16[512,256]{1,0:T(8,128)(2,1)S(1)}, bf16[512,256]{1,0:T(8,128)(2,1)S(1)}, u32[]{:S(2)}, u32[]{:S(2)}) %collective-permute-start.2) | collective-permute-done | bytes 262176 | tf_op jit(solution)/shard_map/ppermute | solution.py:249
  74.3 0.8 %add_multiply_fusion = f32[512,256]{1,0:T(8,128)} fusion(f32[512,256]{1,0:T(8,128)S(1)} %keep.1, bf16[512,256]{1,0:T(8,128)(2,1)S(1)} %collective-permute-done.2), kind=kLoop, calls=%fused_computation.2 | loop fusion | flops 393216 | bytes 1310720 | tf_op jit(solution)/shard_map/mul | solution.py:252
Async XLA Ops:
  2.0 23.0 %all-to-all-start = ((bf16[8,64,1024]{2,1,0:T(8,128)(2,1)}), bf16[8,64,1024]{2,1,0:T(8,128)(2,1)S(1)}, u32[]{:S(2)}, u32[]{:S(2)}) async-start(bf16[8,64,1024]{2,1,0:T(8,128)(2,1)} %spread.1), calls=%async_computation | async-start | bytes 2097152 | tf_op jit(solution)/shard_map/all_to_all | solution.py:25
  19.1 2.6 %collective-permute-start = (bf16[512,512]{1,0:T(8,128)(2,1)S(1)}, bf16[512,512]{1,0:T(8,128)(2,1)S(1)}, u32[]{:S(2)}, u32[]{:S(2)}) collective-permute-start(bf16[512,512]{1,0:T(8,128)(2,1)S(1)} %get-tuple-element.17), channel_id=1, source_target_pairs={{0,8},{8,0},{1,9},{9,1},{2,10},{10,2},{3,11},{11,3},{4,12},{12,4},... | collective-permute-start | bytes 1572872 | tf_op jit(solution)/shard_map/ppermute | solution.py:214
  45.0 3.7 %collective-permute-start.1 = (f32[64,512]{1,0:T(8,128)S(1)}, f32[64,512]{1,0:T(8,128)S(1)}, u32[]{:S(2)}, u32[]{:S(2)}) collective-permute-start(f32[64,512]{1,0:T(8,128)S(1)} %reduce.1.mine_ref), channel_id=1, source_target_pairs={{0,8},{8,0},{1,9},{9,1},{2,10},{10,2},{3,11},{11,3},{4,12},{12,4},... | collective-permute-start | bytes 393224 | tf_op jit(solution)/shard_map/ppermute | solution.py:226
  70.6 3.7 %collective-permute-start.2 = (bf16[512,256]{1,0:T(8,128)(2,1)S(1)}, bf16[512,256]{1,0:T(8,128)(2,1)S(1)}, u32[]{:S(2)}, u32[]{:S(2)}) collective-permute-start(bf16[512,256]{1,0:T(8,128)(2,1)S(1)} %get-tuple-element.22), channel_id=1, source_target_pairs={{0,8},{8,0},{1,9},{9,1},{2,10},{10,2},{3,11},{11,3},{4,12},{12,4},... | collective-permute-start | bytes 786440 | tf_op jit(solution)/shard_map/ppermute | solution.py:249
